TPU v7x, 256 devices: a whole 4x4x8 slice. The times are simulated.
256 devices in a mesh: row: 16 (over x_hi, z), col: 16 (over y, x_lo, core).
Axes of the slice: x: 4 (x_hi: 2, x_lo: 2; x = x_hi * 2 + x_lo), y: 4, z: 8, core: 2. Of those that a mesh axis runs over, the one named last changes fastest.
Arguments:
- panel_values: bfloat16 [65536, 256], P(('row', 'col')), may hold values from -6 to 6
- near_tiles: bfloat16 [8192, 256, 256], P(('row', 'col')), may hold values from -0.01953125 to 0.01953125
- far_left: bfloat16 [32768, 64, 256], P(('row', 'col')), may hold values from -0.0390625 to 0.0390625
- far_right: bfloat16 [32768, 64, 256], P(('row', 'col')), may hold values from -0.375 to 0.375
- near_rows: int32 [8192], P(('row', 'col')), may hold values from 0 to 255, as said below
- far_rows: int32 [32768], P(('row', 'col')), may hold values from 0 to 255, as said below
Outputs:
- panel_product: bfloat16 [65536, 256], P(('row', 'col'))
Inputs may be any that keep to these rules, and one draw needn't show every extreme that they name: `near_rows`: entries of the device at grid position (i, j) lie in its row group, clusters i * 16 * 1 to (i + 1) * 16 - 1. `far_rows`: entries of the device at grid position (i, j) lie in its row group, clusters i * 16 * 1 to (i + 1) * 16 - 1.
All inputs are finite; a program needn't handle non-finite values.
Results may differ from a plain program's by a relative error of at most 0.0046.
Values may be sent and summed in bfloat16 or wider, within the bound.
A program may use at most 192 MiB of HBM per device.

v0:
```python
import jax
import jax.numpy as jnp
from jax import lax
from jax.sharding import PartitionSpec as P

TILE = 256
RANK = 64
NRHS = 256
DPC = 2
LPC = 8


def back_part(near_tiles, far_left, far_right, near_input, far_input, count):
    near_out = jnp.einsum(
        "sij,sin->sjn", near_tiles, near_input, preferred_element_type=jnp.float32
    )
    near_sum = near_out.reshape(count, DPC, TILE, NRHS).sum(axis=1)
    coef = jnp.einsum(
        "skt,stn->skn", far_left, far_input, preferred_element_type=jnp.float32
    ).astype(jnp.bfloat16)
    far_out = jnp.einsum("skt,skn->stn", far_right, coef, preferred_element_type=jnp.float32)
    far_sum = far_out.reshape(count, LPC, TILE, NRHS).sum(axis=1)
    return (near_sum + far_sum).reshape(count * TILE, NRHS)


def forward_part(near_tiles, far_left, far_right, near_local, far_local, colx, count, groups):
    tiles = near_tiles.reshape(count, DPC, TILE, TILE)
    near_out = jnp.einsum("cdij,cjn->cdin", tiles, colx, preferred_element_type=jnp.float32)
    near_out = near_out.reshape(count * DPC, TILE, NRHS)
    right = far_right.reshape(count, LPC, RANK, TILE)
    coef = jnp.einsum("cdkt,ctn->cdkn", right, colx, preferred_element_type=jnp.float32).astype(
        jnp.bfloat16
    )
    left = far_left.reshape(count, LPC, RANK, TILE)
    far_out = jnp.einsum("cdkt,cdkn->cdtn", left, coef, preferred_element_type=jnp.float32)
    far_out = far_out.reshape(count * LPC, TILE, NRHS)
    total = jax.ops.segment_sum(near_out, near_local, num_segments=groups)
    total = total + jax.ops.segment_sum(far_out, far_local, num_segments=groups)
    return total.reshape(groups * TILE, NRHS)


def per_device(panel_values, near_tiles, far_left, far_right, near_rows, far_rows):
    n_row = lax.axis_size("row")
    n_col = lax.axis_size("col")
    clusters = panel_values.shape[0] // TILE
    groups = n_col * clusters
    colcount = n_row * clusters
    row_base = lax.axis_index("row") * groups
    near_local = near_rows - row_base
    far_local = far_rows - row_base
    row_slab = lax.all_gather(panel_values, "col", axis=0, tiled=True)
    rowx = row_slab.reshape(groups, TILE, NRHS)
    near_input = jnp.take(rowx, near_local, axis=0)
    far_input = jnp.take(rowx, far_local, axis=0)
    col_slab = lax.all_gather(panel_values, "row", axis=0, tiled=True)
    colx = col_slab.reshape(colcount, TILE, NRHS)
    forward = forward_part(
        near_tiles, far_left, far_right, near_local, far_local, colx, colcount, groups
    )
    backward = back_part(near_tiles, far_left, far_right, near_input, far_input, colcount)
    own_back = lax.psum_scatter(backward, "row", scatter_dimension=0, tiled=True)
    own_forward = lax.psum_scatter(forward, "col", scatter_dimension=0, tiled=True)
    return (own_forward + own_back).astype(jnp.bfloat16)


def solution(mesh):
    placed = (
        P(("row", "col"), None),
        P(("row", "col"), None, None),
        P(("row", "col"), None, None),
        P(("row", "col"), None, None),
        P(("row", "col")),
        P(("row", "col")),
    )
    return jax.shard_map(
        per_device, mesh=mesh, in_specs=placed, out_specs=P(("row", "col"), None), check_vma=False
    )
```

profile of v0, /device:TPU:2, one launch (start us, length us, event | category | flops | bytes accessed | tf_op | source)
XLA Modules:
  0.0 422.8 jit_solution(15875031635582271066)
XLA Ops:
  6.5 0.7 all-gather.5.cloned.1.call-update
  7.3 0.7 all-gather.3.cloned.1.call-update
  8.1 0.7 compare_and_fusion
  8.7 0.7 compare_and_fusion.1
  9.4 38.9 %all-gather.5.cloned.1.call-done = bf16[4096,256]{1,0:T(8,128)(2,1)} async-done(((bf16[256,256]{1,0:T(8,128)(2,1)}), bf16[4096,256]{1,0:T(8,128)(2,1)}) %all-gather.5.cloned.1.call-update) | async-done | bytes 2097168 | tf_op jit(solution)/shard_map/all_gather | solution.py:51
  48.3 10.0 %gather_fusion.1 = bf16[128,256,256]{2,1,0:T(8,128)(2,1)} fusion(bf16[16,256,256]{2,1,0:T(8,128)(2,1)} %bitcast.32, s32[1024]{0:T(1024)S(1)} %pad_clamp_fusion), kind=kCustom, calls=%fused_computation.1 | custom fusion | bytes 33554944 | tf_op jit(solution)/shard_map/jit(_take)/gather | solution.py:54
  58.4 2.8 gather_fusion
  61.1 7.4 %bitcast_reduce_fusion.1 = f32[16,256,256]{1,2,0:T(8,128)} fusion(bf16[32,256,256]{2,1,0:T(8,128)(2,1)} %param.7, bf16[32,256,256]{2,1,0:T(8,128)(2,1)} %gather_fusion, pred[32]{0:T(512)(128)(4,1)S(1)} %get-tuple-element.7), kind=kOutput, calls=%fused_computation.8 | convolution fusion | flops 1076887552 | bytes 12582944 | tf_op jit(solution)/shard_map/sij,sin->sjn/dot_general | solution.py:14
  68.5 16.6 %bitcast_reduce_fusion = f32[16,256,256]{1,2,0:T(8,128)} fusion(bf16[128,64,256]{2,1,0:T(8,128)(2,1)} %param.9, bf16[128,64,256]{2,1,0:T(8,128)(2,1)} %param.8, bf16[128,256,256]{2,1,0:T(8,128)(2,1)} %gather_fusion.1, pred[128]{0:T(512)(128)(4,1)S(1)} %get-tuple-element.5), kind=kOutput, calls=%fused_computation.4 | convolution fusion | flops 2165309440 | bytes 29360256 | tf_op jit(solution)/shard_map/skt,skn->stn/dot_general | solution.py:21
  85.1 6.0 %add.42 = f32[16,256,256]{1,2,0:T(8,128)} add(f32[16,256,256]{1,2,0:T(8,128)} %bitcast_reduce_fusion.1, f32[16,256,256]{1,2,0:T(8,128)} %bitcast_reduce_fusion) | non-fusion elementwise | flops 1048576 | bytes 12582912 | tf_op jit(solution)/shard_map/add | solution.py:23
  91.1 5.3 %copy.13 = f32[16,256,256]{2,1,0:T(8,128)} copy(f32[16,256,256]{1,2,0:T(8,128)} %add.42) | data formatting | bytes 8388608 | tf_op jit(solution)/shard_map/add | solution.py:23
  96.5 0.2 reduce-scatter.3.cloned.1.call-start
  96.7 39.3 %all-gather.3.cloned.1.call-done = bf16[4096,256]{1,0:T(8,128)(2,1)} async-done(((bf16[256,256]{1,0:T(8,128)(2,1)}), bf16[4096,256]{1,0:T(8,128)(2,1)}) %all-gather.3.cloned.1.call-update) | async-done | bytes 2097168 | tf_op jit(solution)/shard_map/all_gather | solution.py:55
  136.0 16.3 %fusion.16 = f32[16,8,256,256]{3,2,1,0:T(8,128)} fusion(bf16[16,8,64,256]{3,2,1,0:T(8,128)(2,1)} %bitcast.41, bf16[16,8,64,256]{3,2,1,0:T(8,128)(2,1)} %bitcast.40, bf16[16,256,256,1]{2,1,3,0:T(8,128)(2,1)} %bitcast.35), kind=kOutput, calls=%fused_computation.14 | convolution fusion | flops 2149580800 | bytes 44040192 | tf_op jit(solution)/shard_map/cdkt,cdkn->cdtn/dot_general | solution.py:35
  152.3 33.5 %copy.11 = f32[128,256,256]{2,1,0:T(8,128)} copy(f32[128,256,256]{1,2,0:T(8,128)} %bitcast.31) | data formatting | bytes 67108864 | tf_op jit(solution)/shard_map/reshape | solution.py:36
  185.8 2.5 broadcast.9.clone.1
  188.3 72.2 %scatter_fusion.1 = f32[16,256,256]{2,1,0:T(8,128)} fusion(f32[16,256,256]{2,1,0:T(8,128)} %broadcast.9.clone.1, s32[128]{0:T(128)S(1)} %get-tuple-element.6, f32[128,256,256]{2,1,0:T(8,128)} %copy.11), kind=kCustom, calls=%fused_computation.3 | custom fusion | flops 8388608 | bytes 100663808 | tf_op jit(solution)/shard_map/scatter-add | solution.py:38
  260.5 6.7 %fusion.27 = f32[16,2,256,256]{3,2,1,0:T(8,128)} fusion(bf16[16,2,256,256]{3,2,1,0:T(8,128)(2,1)} %bitcast.39, bf16[16,256,256,1]{2,1,3,0:T(8,128)(2,1)S(1)} %bitcast.36), kind=kOutput, calls=%fused_computation.30 | convolution fusion | flops 1073741824 | bytes 14680064 | tf_op jit(solution)/shard_map/cdij,cjn->cdin/dot_general | solution.py:28
  267.2 2.4 broadcast.9.clone
  269.6 18.5 %scatter_fusion = f32[16,256,256]{2,1,0:T(8,128)} fusion(f32[16,256,256]{2,1,0:T(8,128)} %broadcast.9.clone, s32[32]{0:T(128)S(1)} %get-tuple-element.8, f32[32,256,256]{2,1,0:T(8,128)} %bitcast.34), kind=kCustom, calls=%fused_computation.2 | custom fusion | flops 2097152 | bytes 25165952 | tf_op jit(solution)/shard_map/scatter-add | solution.py:37
  288.1 6.1 %add.37 = f32[16,256,256]{2,1,0:T(8,128)} add(f32[16,256,256]{2,1,0:T(8,128)} %scatter_fusion, f32[16,256,256]{2,1,0:T(8,128)} %scatter_fusion.1) | non-fusion elementwise | flops 1048576 | bytes 12582912 | tf_op jit(solution)/shard_map/add | solution.py:38
  294.1 51.0 %reduce-scatter.5.cloned.1.call-done = f32[256,256]{1,0:T(8,128)} async-done(((f32[4096,256]{1,0:T(8,128)}), f32[256,256]{1,0:T(8,128)}) %reduce-scatter.5.cloned.1.call-update) | async-done | bytes 262160 | tf_op jit(solution)/shard_map/reduce_scatter | solution.py:61
  345.1 69.5 %reduce-scatter.3.cloned.1.call-done = f32[256,256]{1,0:T(8,128)} async-done(((f32[4096,256]{1,0:T(8,128)}), f32[256,256]{1,0:T(8,128)}) %reduce-scatter.3.cloned.1.call-update) | async-done | bytes 262160 | tf_op jit(solution)/shard_map/reduce_scatter | solution.py:62
  414.6 1.7 add_convert_fusion
  (13 shorter events, 0.1 us)
Async XLA Ops:
  6.5 41.8 %all-gather.5.cloned.1.call-start = ((), (), s32[]{:S(2)}) async-start(), calls=%async_computation.4 | async-start | bytes 2228224 | tf_op jit(solution)/shard_map/all_gather | solution.py:51
  7.3 128.7 %all-gather.3.cloned.1.call-start = ((), (), s32[]{:S(2)}) async-start(), calls=%async_computation.2 | async-start | bytes 2228224 | tf_op jit(solution)/shard_map/all_gather | solution.py:55
  8.0 337.1 %reduce-scatter.5.cloned.1.call-start = ((), (), s32[]{:S(2)}) async-start(), calls=%async_computation.5 | async-start | bytes 4456448 | tf_op jit(solution)/shard_map/reduce_scatter | solution.py:61
  48.3 10.0 %copy-start = (bf16[4096,256]{1,0:T(8,128)(2,1)S(1)}, bf16[4096,256]{1,0:T(8,128)(2,1)}, u32[]{:S(2)}) copy-start(bf16[4096,256]{1,0:T(8,128)(2,1)} %all-gather.5.cloned.1.call-done) | copy-start | bytes 6291460
  96.5 318.1 %reduce-scatter.3.cloned.1.call-start = ((), (), s32[]{:S(2)}) async-start(), calls=%async_computation.3 | async-start | bytes 4456448 | tf_op jit(solution)/shard_map/reduce_scatter | solution.py:62
  188.3 72.2 %copy-start.1 = (bf16[4096,256]{1,0:T(8,128)(2,1)S(1)}, bf16[4096,256]{1,0:T(8,128)(2,1)}, u32[]{:S(2)}) copy-start(bf16[4096,256]{1,0:T(8,128)(2,1)} %all-gather.3.cloned.1.call-done) | copy-start | bytes 6291460
Sparse Core Ops, SparseCore 0:
  9.2 39.0 all-gather.4
  50.9 84.9 all-gather.2
  140.0 205.0 reduce-scatter.4
  347.7 66.8 reduce-scatter.2
where the time goes:
time: 427 us; the launch traced here: 423 us
  waiting for transfers between devices  200 us (47%)
  other arithmetic  106 us (25%)
  local copies, waits for them, and re-layouts  56.6 us (13%)
  matrix products  46.9 us (11%)
  between operations  13.2 us (3%)
    scatter-add x1, other arithmetic, forward_part(): total = total + jax.ops.segment_sum(far_out, far_local, num_segments=groups)  72.2 us
    reduce_scatter x1, waiting for transfers between devices, per_device(): lax.psum_scatter(forward, 'col', scatter_dimension=0, tiled=True)  69.5 us
    reduce_scatter x1, waiting for transfers between devices, per_device(): lax.psum_scatter(backward, 'row', scatter_dimension=0, tiled=True)  51 us
    all_gather x1, waiting for transfers between devices, per_device(): col_slab = lax.all_gather(panel_values, 'row', axis=0, tiled=True)  39.3 us
    all_gather x1, waiting for transfers between devices, per_device(): row_slab = lax.all_gather(panel_values, 'col', axis=0, tiled=True)  38.9 us
    reshape x1, local copies, waits for them, and re-layouts, forward_part(): far_out = far_out.reshape(count * LPC, TILE, NRHS)  33.5 us
    scatter-add x1, other arithmetic, forward_part(): total = jax.ops.segment_sum(near_out, near_local, num_segments=groups)  18.5 us
    dot_general x1, matrix products, back_part(): jnp.einsum('skt,skn->stn', far_right, coef, preferred_element_type=jnp.fl...  16.6 us
  transfers between devices with their start and end apart: 4, of which 4 were waited for; matrix products, arithmetic and copies ran while one was open for 49% of the time, Pallas kernels for 0%

commit v1 on v0

v1 whole, which is shorter than its diff:
```python
import jax
import jax.numpy as jnp
from jax import lax
from jax.experimental import pallas as pl
from jax.experimental.pallas import tpu as pltpu
from jax.sharding import PartitionSpec as P

TILE = 256
RANK = 64
NRHS = 256
DPC = 2
LPC = 8

TN = (((0,), (0,)), ((), ()))


def local_kernel(near_idx, far_idx, tiles_ref, left_ref, right_ref, colx_ref, rowx_ref, f_ref, b_ref):
    k = pl.program_id(0)

    @pl.when(k == 0)
    def _():
        f_ref[...] = jnp.zeros_like(f_ref)

    xc = colx_ref[0]
    acc = jnp.zeros((TILE, NRHS), jnp.float32)
    for d in range(DPC):
        r = near_idx[k * DPC + d]
        t = tiles_ref[d]
        f_ref[r] += jnp.dot(t, xc, preferred_element_type=jnp.float32)
        acc += lax.dot_general(t, rowx_ref[r], TN, preferred_element_type=jnp.float32)
    for d in range(LPC):
        r = far_idx[k * LPC + d]
        right = right_ref[d]
        left = left_ref[d]
        coef = jnp.dot(right, xc, preferred_element_type=jnp.float32).astype(jnp.bfloat16)
        f_ref[r] += lax.dot_general(left, coef, TN, preferred_element_type=jnp.float32)
        tcoef = jnp.dot(left, rowx_ref[r], preferred_element_type=jnp.float32).astype(jnp.bfloat16)
        acc += lax.dot_general(right, tcoef, TN, preferred_element_type=jnp.float32)
    b_ref[0] = acc


def local_products(near_local, far_local, near_tiles, far_left, far_right, colx, rowx):
    count = colx.shape[0]
    groups = rowx.shape[0]
    grid_spec = pltpu.PrefetchScalarGridSpec(
        num_scalar_prefetch=2,
        grid=(count,),
        in_specs=[
            pl.BlockSpec((DPC, TILE, TILE), lambda k, a, b: (k, 0, 0)),
            pl.BlockSpec((LPC, RANK, TILE), lambda k, a, b: (k, 0, 0)),
            pl.BlockSpec((LPC, RANK, TILE), lambda k, a, b: (k, 0, 0)),
            pl.BlockSpec((1, TILE, NRHS), lambda k, a, b: (k, 0, 0)),
            pl.BlockSpec((groups, TILE, NRHS), lambda k, a, b: (0, 0, 0)),
        ],
        out_specs=[
            pl.BlockSpec((groups, TILE, NRHS), lambda k, a, b: (0, 0, 0)),
            pl.BlockSpec((1, TILE, NRHS), lambda k, a, b: (k, 0, 0)),
        ],
    )
    flops = 2 * TILE * TILE * NRHS * near_tiles.shape[0] * 2 + 2 * RANK * TILE * NRHS * far_left.shape[0] * 4
    return pl.pallas_call(
        local_kernel,
        grid_spec=grid_spec,
        out_shape=[
            jax.ShapeDtypeStruct((groups, TILE, NRHS), jnp.float32),
            jax.ShapeDtypeStruct((count, TILE, NRHS), jnp.float32),
        ],
        compiler_params=pltpu.CompilerParams(
            dimension_semantics=("arbitrary",), vmem_limit_bytes=48 * 1024 * 1024
        ),
        cost_estimate=pl.CostEstimate(flops=flops, bytes_accessed=24 * 1024 * 1024, transcendentals=0),
    )(near_local, far_local, near_tiles, far_left, far_right, colx, rowx)


def per_device(panel_values, near_tiles, far_left, far_right, near_rows, far_rows):
    n_row = lax.axis_size("row")
    n_col = lax.axis_size("col")
    clusters = panel_values.shape[0] // TILE
    groups = n_col * clusters
    colcount = n_row * clusters
    row_base = lax.axis_index("row") * groups
    near_local = near_rows - row_base
    far_local = far_rows - row_base
    row_slab = lax.all_gather(panel_values, "col", axis=0, tiled=True)
    rowx = row_slab.reshape(groups, TILE, NRHS)
    col_slab = lax.all_gather(panel_values, "row", axis=0, tiled=True)
    colx = col_slab.reshape(colcount, TILE, NRHS)
    forward, backward = local_products(near_local, far_local, near_tiles, far_left, far_right, colx, rowx)
    own_back = lax.psum_scatter(backward.reshape(colcount * TILE, NRHS), "row", scatter_dimension=0, tiled=True)
    own_forward = lax.psum_scatter(forward.reshape(groups * TILE, NRHS), "col", scatter_dimension=0, tiled=True)
    return (own_forward + own_back).astype(jnp.bfloat16)


def solution(mesh):
    placed = (
        P(("row", "col"), None),
        P(("row", "col"), None, None),
        P(("row", "col"), None, None),
        P(("row", "col"), None, None),
        P(("row", "col")),
        P(("row", "col")),
    )
    return jax.shard_map(
        per_device, mesh=mesh, in_specs=placed, out_specs=P(("row", "col"), None), check_vma=False
    )
```

time: 427 us -> 465 us (1.089)
  waiting for transfers between devices: 200 us -> 402 us
  other arithmetic: 106 us -> 3.03 us
  local copies, waits for them, and re-layouts: 56.6 us -> 3.18 us
  matrix products: 46.9 us -> 0 us
  Pallas kernels: 0 us -> 38.8 us
    reduce_scatter x2, waiting for transfers between devices: 120 us -> 277 us  [the longest x1 208 us: per_device(): lax.psum_scatter(backward.reshape(colcount * TILE, NRHS), 'row', scatter_...]
    scatter-add x2 -> x0, other arithmetic: 90.7 us -> none  [the longest x1 72.2 us: forward_part(): total = total + jax.ops.segment_sum(far_out, far_local, num_segments=groups)]
    all_gather x1, waiting for transfers between devices: 39.3 us -> 88.1 us  [per_device(): col_slab = lax.all_gather(panel_values, 'row', axis=0, tiled=True)]
    dot_general x4 -> x0, matrix products: 46.9 us -> none  [the longest x1 16.6 us: back_part(): jnp.einsum('skt,skn->stn', far_right, coef, preferred_element_type=jnp.fl...]
    pallas_call x0 -> x1, Pallas kernels: none -> 38.8 us  [local_products(): pl.pallas_call(local_kernel, grid_spec=grid_spec, out_shape=[jax.ShapeDty...]
    reshape x1 -> x0, local copies, waits for them, and re-layouts: 33.5 us -> none  [forward_part(): far_out = far_out.reshape(count * LPC, TILE, NRHS)]
    gather x2 -> x0, local copies, waits for them, and re-layouts: 12.8 us -> none  [the longest x1 10 us: per_device(): far_input = jnp.take(rowx, far_local, axis=0)]
    add x2 -> x0, other arithmetic: 12.1 us -> none  [the longest x1 6.05 us: forward_part(): total = total + jax.ops.segment_sum(far_out, far_local, num_segments=groups)]
  transfers between devices with their start and end apart: 4 -> 4, of which waited for: 4 -> 4; matrix products, arithmetic and copies ran while one was open for 49% -> 0% of each run, Pallas kernels for 0% -> 0%
where the time goes in v1:
time: 465 us; the launch traced here: 461 us
  waiting for transfers between devices  402 us (86%)
  Pallas kernels  38.8 us (8%)
  between operations  13.1 us (3%)
    reduce_scatter x1, waiting for transfers between devices, per_device(): lax.psum_scatter(backward.reshape(colcount * TILE, NRHS), 'row', scatter_...  208 us
    all_gather x1, waiting for transfers between devices, per_device(): col_slab = lax.all_gather(panel_values, 'row', axis=0, tiled=True)  88.1 us
    reduce_scatter x1, waiting for transfers between devices, per_device(): lax.psum_scatter(forward.reshape(groups * TILE, NRHS), 'col', scatter_dim...  69 us
    pallas_call x1, Pallas kernels, local_products(): pl.pallas_call(local_kernel, grid_spec=grid_spec, out_shape=[jax.ShapeDty...  38.8 us
    all_gather x1, waiting for transfers between devices, per_device(): row_slab = lax.all_gather(panel_values, 'col', axis=0, tiled=True)  35.6 us
  transfers between devices with their start and end apart: 4, of which 4 were waited for; matrix products, arithmetic and copies ran while one was open for 0% of the time, Pallas kernels for 0%

profile of v1, /device:TPU:2, one launch (start us, length us, event | category | flops | bytes accessed | tf_op | source)
XLA Modules:
  0.0 460.7 jit_solution(5550201478532062057)
XLA Ops:
  6.5 0.0 all-gather.3.cloned.1.call-start
  6.5 0.7 all-gather.3.cloned.1.call-update
  7.3 0.0 all-gather.5.cloned.1.call-start
  7.3 0.7 all-gather.5.cloned.1.call-update
  8.0 0.0 reduce-scatter.5.cloned.1.call-start
  8.1 0.7 broadcast_subtract_fusion.1.near_idx
  8.7 0.7 broadcast_subtract_fusion.far_idx
  9.4 88.1 %all-gather.3.cloned.1.call-done = bf16[4096,256]{1,0:T(8,128)(2,1)} async-done(((bf16[256,256]{1,0:T(8,128)(2,1)}), bf16[4096,256]{1,0:T(8,128)(2,1)}) %all-gather.3.cloned.1.call-update) | async-done | bytes 2097168 | tf_op jit(solution)/shard_map/all_gather | solution.py:86
  97.5 35.6 %all-gather.5.cloned.1.call-done = bf16[4096,256]{1,0:T(8,128)(2,1)} async-done(((bf16[256,256]{1,0:T(8,128)(2,1)}), bf16[4096,256]{1,0:T(8,128)(2,1)}) %all-gather.5.cloned.1.call-update) | async-done | bytes 2097168 | tf_op jit(solution)/shard_map/all_gather | solution.py:84
  133.1 0.0 copy-start
  133.1 1.6 copy-done
  134.7 0.0 copy-start.1
  134.7 1.6 copy-done.1
  136.3 38.8 %shard_map.64 = (f32[16,256,256]{2,1,0:T(8,128)}, f32[16,256,256]{2,1,0:T(8,128)}) custom-call(s32[32]{0:T(128)S(1)} %broadcast_subtract_fusion.1.near_idx, s32[128]{0:T(128)S(1)} %broadcast_subtract_fusion.far_idx, bf16[32,256,256]{2,1,0:T(8,128)(2,1)} %tiles_ref.1, bf16[128,64,256]{2,1,0:T(8,128)(2,1)} %left_ref.1, bf16[128,64,256]{2,1,0:T(8,128)(2,1)} %right_ref.1, ...), custom_call_target="tpu_custom_call" | custom-call | flops 6442450944 | bytes 25165824 | tf_op jit(solution)/shard_map/pallas_call | solution.py:61
  175.1 0.0 reduce-scatter.5.cloned.1.call-update
  175.1 0.0 reduce-scatter.3.cloned.1.call-start
  175.2 0.5 reduce-scatter.3.cloned.1.call-update
  175.7 207.7 %reduce-scatter.5.cloned.1.call-done = f32[256,256]{1,0:T(8,128)} async-done(((f32[4096,256]{1,0:T(8,128)}), f32[256,256]{1,0:T(8,128)}) %reduce-scatter.5.cloned.1.call-update) | async-done | bytes 262160 | tf_op jit(solution)/shard_map/reduce_scatter | solution.py:89
  383.4 69.0 %reduce-scatter.3.cloned.1.call-done = f32[256,256]{1,0:T(8,128)} async-done(((f32[4096,256]{1,0:T(8,128)}), f32[256,256]{1,0:T(8,128)}) %reduce-scatter.3.cloned.1.call-update) | async-done | bytes 262160 | tf_op jit(solution)/shard_map/reduce_scatter | solution.py:90
  452.4 1.7 add_convert_fusion
Async XLA Ops:
  6.5 91.0 %all-gather.3.cloned.1.call-start = ((), (), s32[]{:S(2)}) async-start(), calls=%async_computation.2 | async-start | bytes 2228224 | tf_op jit(solution)/shard_map/all_gather | solution.py:86
  7.3 125.8 %all-gather.5.cloned.1.call-start = ((), (), s32[]{:S(2)}) async-start(), calls=%async_computation.3 | async-start | bytes 2228224 | tf_op jit(solution)/shard_map/all_gather | solution.py:84
  8.0 375.4 %reduce-scatter.5.cloned.1.call-start = ((), (), s32[]{:S(2)}) async-start(), calls=%async_computation.5 | async-start | bytes 4456448 | tf_op jit(solution)/shard_map/reduce_scatter | solution.py:89
  133.1 1.6 copy-start
  134.7 1.6 copy-start.1
  175.1 277.3 %reduce-scatter.3.cloned.1.call-start = ((), (), s32[]{:S(2)}) async-start(), calls=%async_computation.4 | async-start | bytes 4456448 | tf_op jit(solution)/shard_map/reduce_scatter | solution.py:90
Sparse Core Ops, SparseCore 0:
  9.9 87.5 all-gather.2
  99.4 33.6 all-gather.4
  175.3 208.0 reduce-scatter.4
  386.0 66.4 reduce-scatter.2

commit v2 on v1

--- a/solution.py
+++ b/solution.py
@@ -1,3 +1,5 @@
+import functools
+
 import jax
 import jax.numpy as jnp
 from jax import lax
@@ -72,6 +74,118 @@
     )(near_local, far_local, near_tiles, far_left, far_right, colx, rowx)
 
 
+MESH_ID = pl.DeviceIdType.MESH
+
+
+def peers(nr, nc):
+    i = lax.axis_index("row")
+    j = lax.axis_index("col")
+    cols = [(i, lax.rem(j + o, nc)) for o in range(1, nc)]
+    rows = [(lax.rem(i + o, nr), j) for o in range(1, nr)]
+    return i, j, cols, rows
+
+
+def enter(cols, rows):
+    barrier = pltpu.get_barrier_semaphore()
+    for dev in cols + rows:
+        pl.semaphore_signal(barrier, 1, device_id=dev, device_id_type=MESH_ID)
+    pl.semaphore_wait(barrier, len(cols) + len(rows))
+
+
+def gather_kernel(nr, nc, x_ref, rowx_ref, colx_ref, send_sem, recv_sem, local_sem):
+    i, j, cols, rows = peers(nr, nc)
+    enter(cols, rows)
+    copies = []
+    for n, dev in enumerate(cols):
+        copies.append(pltpu.make_async_remote_copy(
+            x_ref, rowx_ref.at[j], send_sem.at[n], recv_sem.at[n], device_id=dev, device_id_type=MESH_ID))
+    for n, dev in enumerate(rows):
+        q = len(cols) + n
+        copies.append(pltpu.make_async_remote_copy(
+            x_ref, colx_ref.at[i], send_sem.at[q], recv_sem.at[q], device_id=dev, device_id_type=MESH_ID))
+    for c in copies:
+        c.start()
+    own_row = pltpu.make_async_copy(x_ref, rowx_ref.at[j], local_sem.at[0])
+    own_col = pltpu.make_async_copy(x_ref, colx_ref.at[i], local_sem.at[1])
+    own_row.start()
+    own_col.start()
+    for c in copies:
+        c.wait()
+    own_row.wait()
+    own_col.wait()
+
+
+def gather_slabs(x, nr, nc):
+    tile = x.shape
+    peers_n = nr + nc - 2
+    return pl.pallas_call(
+        functools.partial(gather_kernel, nr, nc),
+        out_shape=[
+            jax.ShapeDtypeStruct((nc,) + tile, x.dtype),
+            jax.ShapeDtypeStruct((nr,) + tile, x.dtype),
+        ],
+        in_specs=[pl.BlockSpec(memory_space=pl.ANY)],
+        out_specs=[pl.BlockSpec(memory_space=pl.ANY)] * 2,
+        scratch_shapes=[
+            pltpu.SemaphoreType.DMA((peers_n,)),
+            pltpu.SemaphoreType.DMA((peers_n,)),
+            pltpu.SemaphoreType.DMA((2,)),
+        ],
+        compiler_params=pltpu.CompilerParams(collective_id=0, has_side_effects=True),
+    )(x)
+
+
+def scatter_kernel(nr, nc, f_ref, b_ref, out_ref, recv_f, recv_b, send_sem, recv_sem, local_sem):
+    i, j, cols, rows = peers(nr, nc)
+    enter(cols, rows)
+    copies = []
+    for n, dev in enumerate(cols):
+        copies.append(pltpu.make_async_remote_copy(
+            f_ref.at[dev[1]], recv_f.at[n + 1], send_sem.at[n], recv_sem.at[n],
+            device_id=dev, device_id_type=MESH_ID))
+    for n, dev in enumerate(rows):
+        q = len(cols) + n
+        copies.append(pltpu.make_async_remote_copy(
+            b_ref.at[dev[0]], recv_b.at[n + 1], send_sem.at[q], recv_sem.at[q],
+            device_id=dev, device_id_type=MESH_ID))
+    for c in copies:
+        c.start()
+    own_f = pltpu.make_async_copy(f_ref.at[j], recv_f.at[0], local_sem.at[0])
+    own_b = pltpu.make_async_copy(b_ref.at[i], recv_b.at[0], local_sem.at[1])
+    own_f.start()
+    own_b.start()
+    for c in copies:
+        c.wait()
+    own_f.wait()
+    own_b.wait()
+    acc = recv_f[0] + recv_b[0]
+    for n in range(1, nc):
+        acc = acc + recv_f[n]
+    for n in range(1, nr):
+        acc = acc + recv_b[n]
+    out_ref[...] = acc.astype(out_ref.dtype)
+
+
+def scatter_sum(forward, backward, nr, nc):
+    tile = forward.shape[1:]
+    peers_n = nr + nc - 2
+    return pl.pallas_call(
+        functools.partial(scatter_kernel, nr, nc),
+        out_shape=jax.ShapeDtypeStruct(tile, jnp.bfloat16),
+        in_specs=[pl.BlockSpec(memory_space=pl.ANY)] * 2,
+        out_specs=pl.BlockSpec(memory_space=pltpu.VMEM),
+        scratch_shapes=[
+            pltpu.VMEM((nc,) + tile, jnp.float32),
+            pltpu.VMEM((nr,) + tile, jnp.float32),
+            pltpu.SemaphoreType.DMA((peers_n,)),
+            pltpu.SemaphoreType.DMA((peers_n,)),
+            pltpu.SemaphoreType.DMA((2,)),
+        ],
+        compiler_params=pltpu.CompilerParams(
+            collective_id=1, has_side_effects=True, vmem_limit_bytes=32 * 1024 * 1024),
+    )(forward, backward)
+
+
 def per_device(panel_values, near_tiles, far_left, far_right, near_rows, far_rows):
     n_row = lax.axis_size("row")
     n_col = lax.axis_size("col")
@@ -81,14 +195,9 @@
     row_base = lax.axis_index("row") * groups
     near_local = near_rows - row_base
     far_local = far_rows - row_base
-    row_slab = lax.all_gather(panel_values, "col", axis=0, tiled=True)
-    rowx = row_slab.reshape(groups, TILE, NRHS)
-    col_slab = lax.all_gather(panel_values, "row", axis=0, tiled=True)
-    colx = col_slab.reshape(colcount, TILE, NRHS)
+    rowx, colx = gather_slabs(panel_values, n_row, n_col)
     forward, backward = local_products(near_local, far_local, near_tiles, far_left, far_right, colx, rowx)
-    own_back = lax.psum_scatter(backward.reshape(colcount * TILE, NRHS), "row", scatter_dimension=0, tiled=True)
-    own_forward = lax.psum_scatter(forward.reshape(groups * TILE, NRHS), "col", scatter_dimension=0, tiled=True)
-    return (own_forward + own_back).astype(jnp.bfloat16)
+    return scatter_sum(forward, backward, n_row, n_col)
 
 
 def solution(mesh):

time: 465 us -> 215 us (0.46)
  the two profiles are of different devices: /device:TPU:2 before, /device:TPU:1 now
where the time goes in v2:
time: 215 us
  Pallas kernels  205 us (95%)
  local copies, waits for them, and re-layouts  8.21 us (4%)
    pallas_call x1, Pallas kernels, scatter_sum(): pl.pallas_call(functools.partial(scatter_kernel, nr, nc), out_shape=jax.S...  107 us
    pallas_call x1, Pallas kernels, gather_slabs(): pl.pallas_call(functools.partial(gather_kernel, nr, nc), out_shape=[jax.S...  59.4 us
    pallas_call x1, Pallas kernels, local_products(): pl.pallas_call(local_kernel, grid_spec=grid_spec, out_shape=[jax.ShapeDty...  38.8 us
    unnamed x9, local copies, waits for them, and re-layouts  8.21 us

profile of v2, /device:TPU:1, one launch (start us, length us, event | category | flops | bytes accessed | tf_op | source)
XLA Modules:
  0.0 214.8 jit_solution(10891662223827544046)
XLA Ops:
  0.0 0.7 broadcast_subtract_fusion.1.near_idx
  0.7 0.7 broadcast_subtract_fusion.far_idx
  1.3 59.4 %shard_map.64 = (bf16[16,256,256]{2,1,0:T(8,128)(2,1)}, bf16[16,256,256]{2,1,0:T(8,128)(2,1)}) custom-call(bf16[256,256]{1,0:T(8,128)(2,1)} %x_ref.1), custom_call_target="tpu_custom_call" | custom-call | tf_op jit(solution)/shard_map/pallas_call | solution.py:121
  60.7 0.0 copy-start.2
  60.7 1.6 copy-done.2
  62.3 0.0 copy-start.3
  62.3 1.6 copy-done.3
  63.9 38.8 %shard_map.65 = (f32[16,256,256]{2,1,0:T(8,128)}, f32[16,256,256]{2,1,0:T(8,128)}) custom-call(s32[32]{0:T(128)S(1)} %broadcast_subtract_fusion.1.near_idx, s32[128]{0:T(128)S(1)} %broadcast_subtract_fusion.far_idx, bf16[32,256,256]{2,1,0:T(8,128)(2,1)} %tiles_ref.1, bf16[128,64,256]{2,1,0:T(8,128)(2,1)} %left_ref.1, bf16[128,64,256]{2,1,0:T(8,128)(2,1)} %right_ref.1, ...), custom_call_target="tpu_custom_call" | custom-call | flops 6442450944 | bytes 25165824 | tf_op jit(solution)/shard_map/pallas_call | solution.py:63
  102.7 0.0 copy-start
  102.7 2.2 %copy-done = f32[16,256,256]{2,1,0:T(8,128)S(1)} copy-done((f32[16,256,256]{2,1,0:T(8,128)S(1)}, f32[16,256,256]{2,1,0:T(8,128)}, u32[]{:S(2)}) %copy-start) | copy-done | bytes 4194328
  104.9 0.0 copy-start.1
  104.9 2.2 %copy-done.1 = f32[16,256,256]{2,1,0:T(8,128)S(1)} copy-done((f32[16,256,256]{2,1,0:T(8,128)S(1)}, f32[16,256,256]{2,1,0:T(8,128)}, u32[]{:S(2)}) %copy-start.1) | copy-done | bytes 4194328
  107.1 107.1 %shard_map.66 = bf16[256,256]{1,0:T(8,128)(2,1)S(1)} custom-call(f32[16,256,256]{2,1,0:T(8,128)S(1)} %copy-done, f32[16,256,256]{2,1,0:T(8,128)S(1)} %copy-done.1), custom_call_target="tpu_custom_call" | custom-call | tf_op jit(solution)/shard_map/pallas_call | solution.py:172
  214.2 0.7 copy.8
Async XLA Ops:
  60.7 1.6 copy-start.2
  62.3 1.6 copy-start.3
  102.7 2.2 %copy-start = (f32[16,256,256]{2,1,0:T(8,128)S(1)}, f32[16,256,256]{2,1,0:T(8,128)}, u32[]{:S(2)}) copy-start(f32[16,256,256]{2,1,0:T(8,128)} %get-tuple-element.11.f_ref) | copy-start | bytes 12582916
  104.9 2.2 %copy-start.1 = (f32[16,256,256]{2,1,0:T(8,128)S(1)}, f32[16,256,256]{2,1,0:T(8,128)}, u32[]{:S(2)}) copy-start(f32[16,256,256]{2,1,0:T(8,128)} %get-tuple-element.12.b_ref) | copy-start | bytes 12582916

commit v3 on v1

--- a/solution.py
+++ b/solution.py
@@ -1,3 +1,5 @@
+import functools
+
 import jax
 import jax.numpy as jnp
 from jax import lax
@@ -72,6 +74,177 @@
     )(near_local, far_local, near_tiles, far_left, far_right, colx, rowx)
 
 
+MESH_ID = pl.DeviceIdType.MESH
+
+
+def layout(nr, nc):
+    i = lax.axis_index("row")
+    j = lax.axis_index("col")
+    half = nr // 2
+    xh = i // half
+    z = lax.rem(i, half)
+    cols = [(i, lax.rem(j + o, nc)) for o in range(1, nc)]
+    right = (xh * half + lax.rem(z + 1, half), j)
+    left = (xh * half + lax.rem(z + half - 1, half), j)
+    partner = (lax.rem(i + half, nr), j)
+    return i, j, half, xh, z, cols, right, left, partner
+
+
+def enter(devices):
+    barrier = pltpu.get_barrier_semaphore()
+    for dev in devices:
+        pl.semaphore_signal(barrier, 1, device_id=dev, device_id_type=MESH_ID)
+    pl.semaphore_wait(barrier, len(devices))
+
+
+def remote(src, dst, ssem, rsem, dev):
+    return pltpu.make_async_remote_copy(src, dst, ssem, rsem, device_id=dev, device_id_type=MESH_ID)
+
+
+def gather_kernel(nr, nc, x_ref, rowx_ref, colx_ref, col_send, col_recv, ring_send, ring_recv, local_sem):
+    i, j, half, xh, z, cols, right, left, partner = layout(nr, nc)
+    cw = half // 2
+    ccw = half - 1 - cw
+    enter(cols + [right, left, partner])
+    col_copies = [remote(x_ref, rowx_ref.at[j], col_send.at[n], col_recv.at[n], dev) for n, dev in enumerate(cols)]
+    for c in col_copies:
+        c.start()
+    other = remote(x_ref, colx_ref.at[xh, z], ring_send.at[0], ring_recv.at[0], partner)
+    other.start()
+    own_row = pltpu.make_async_copy(x_ref, rowx_ref.at[j], local_sem.at[0])
+    own_col = pltpu.make_async_copy(x_ref, colx_ref.at[xh, z], local_sem.at[1])
+    own_row.start()
+    own_col.start()
+    own_col.wait()
+    other.wait()
+    ring = []
+    prev_cw = prev_ccw = None
+    for t in range(1, cw + 1):
+        origin = lax.rem(z - t + 1 + half, half)
+        if prev_cw is not None:
+            prev_cw.wait_recv()
+        c = remote(colx_ref.at[:, origin], colx_ref.at[:, origin], ring_send.at[t], ring_recv.at[t], right)
+        c.start()
+        ring.append(c)
+        prev_cw = c
+        if t <= ccw:
+            origin = lax.rem(z + t - 1, half)
+            if prev_ccw is not None:
+                prev_ccw.wait_recv()
+            c = remote(colx_ref.at[:, origin], colx_ref.at[:, origin], ring_send.at[cw + t],
+                       ring_recv.at[cw + t], left)
+            c.start()
+            ring.append(c)
+            prev_ccw = c
+    for c in ring:
+        c.wait_send()
+    prev_cw.wait_recv()
+    prev_ccw.wait_recv()
+    for c in col_copies:
+        c.wait()
+    own_row.wait()
+
+
+def gather_slabs(x, nr, nc):
+    tile = x.shape
+    half = nr // 2
+    return pl.pallas_call(
+        functools.partial(gather_kernel, nr, nc),
+        out_shape=[
+            jax.ShapeDtypeStruct((nc,) + tile, x.dtype),
+            jax.ShapeDtypeStruct((2, half) + tile, x.dtype),
+        ],
+        in_specs=[pl.BlockSpec(memory_space=pl.ANY)],
+        out_specs=[pl.BlockSpec(memory_space=pl.ANY)] * 2,
+        scratch_shapes=[
+            pltpu.SemaphoreType.DMA((nc - 1,)),
+            pltpu.SemaphoreType.DMA((nc - 1,)),
+            pltpu.SemaphoreType.DMA((half,)),
+            pltpu.SemaphoreType.DMA((half,)),
+            pltpu.SemaphoreType.DMA((2,)),
+        ],
+        compiler_params=pltpu.CompilerParams(collective_id=0, has_side_effects=True),
+    )(x)
+
+
+def scatter_kernel(nr, nc, f_ref, b_ref, out_ref, recv_f, ring_in, ring_out, x_in, x_out,
+                   col_send, col_recv, ring_send, ring_recv, local_sem):
+    i, j, half, xh, z, cols, right, left, partner = layout(nr, nc)
+    cw = half // 2
+    ccw = half - 1 - cw
+    enter(cols + [right, left, partner])
+    col_copies = [
+        remote(f_ref.at[dev[1]], recv_f.at[n + 1], col_send.at[n], col_recv.at[n], dev) for n, dev in enumerate(cols)
+    ]
+    for c in col_copies:
+        c.start()
+    sends = []
+    arrivals = {}
+    for t in range(1, cw + 1):
+        for way in range(2):
+            if way == 1 and t > ccw:
+                continue
+            if way == 0:
+                target = lax.rem(z + cw + 1 - t, half)
+                slot, dev = t - 1, right
+            else:
+                target = lax.rem(z + half - (ccw + 1 - t), half)
+                slot, dev = cw + t - 1, left
+            if t == 1:
+                src = b_ref.at[:, target]
+            else:
+                arrivals[(way, t - 1)].wait_recv()
+                ring_out[slot] = ring_in[slot - 1] + b_ref[:, target]
+                src = ring_out.at[slot]
+            c = remote(src, ring_in.at[slot], ring_send.at[slot], ring_recv.at[slot], dev)
+            c.start()
+            sends.append(c)
+            arrivals[(way, t)] = c
+    arrivals[(0, cw)].wait_recv()
+    arrivals[(1, ccw)].wait_recv()
+    away = 1 - xh
+    x_out[...] = ring_in[cw - 1, away] + ring_in[cw + ccw - 1, away] + b_ref[away, z]
+    cross = remote(x_out, x_in, ring_send.at[half - 1], ring_recv.at[half - 1], partner)
+    cross.start()
+    for c in sends:
+        c.wait_send()
+    for c in col_copies:
+        c.wait()
+    cross.wait()
+    acc = ring_in[cw - 1, xh] + ring_in[cw + ccw - 1, xh] + b_ref[xh, z] + x_in[...] + f_ref[j]
+    for n in range(1, nc):
+        acc = acc + recv_f[n]
+    out_ref[...] = acc.astype(out_ref.dtype)
+
+
+def scatter_sum(forward, backward, nr, nc):
+    tile = forward.shape[1:]
+    half = nr // 2
+    cw = half // 2
+    steps = half - 1
+    vmem = pltpu.VMEM
+    return pl.pallas_call(
+        functools.partial(scatter_kernel, nr, nc),
+        out_shape=jax.ShapeDtypeStruct(tile, jnp.bfloat16),
+        in_specs=[pl.BlockSpec(memory_space=vmem)] * 2,
+        out_specs=pl.BlockSpec(memory_space=vmem),
+        scratch_shapes=[
+            vmem((nc,) + tile, jnp.float32),
+            vmem((steps, 2) + tile, jnp.float32),
+            vmem((steps, 2) + tile, jnp.float32),
+            vmem(tile, jnp.float32),
+            vmem(tile, jnp.float32),
+            pltpu.SemaphoreType.DMA((nc - 1,)),
+            pltpu.SemaphoreType.DMA((nc - 1,)),
+            pltpu.SemaphoreType.DMA((half,)),
+            pltpu.SemaphoreType.DMA((half,)),
+            pltpu.SemaphoreType.DMA((2,)),
+        ],
+        compiler_params=pltpu.CompilerParams(
+            collective_id=1, has_side_effects=True, vmem_limit_bytes=48 * 1024 * 1024),
+    )(forward, backward.reshape((2, half) + tile))
+
+
 def per_device(panel_values, near_tiles, far_left, far_right, near_rows, far_rows):
     n_row = lax.axis_size("row")
     n_col = lax.axis_size("col")
@@ -81,14 +254,10 @@
     row_base = lax.axis_index("row") * groups
     near_local = near_rows - row_base
     far_local = far_rows - row_base
-    row_slab = lax.all_gather(panel_values, "col", axis=0, tiled=True)
-    rowx = row_slab.reshape(groups, TILE, NRHS)
-    col_slab = lax.all_gather(panel_values, "row", axis=0, tiled=True)
-    colx = col_slab.reshape(colcount, TILE, NRHS)
+    rowx, colx = gather_slabs(panel_values, n_row, n_col)
+    colx = colx.reshape(colcount, TILE, NRHS)
     forward, backward = local_products(near_local, far_local, near_tiles, far_left, far_right, colx, rowx)
-    own_back = lax.psum_scatter(backward.reshape(colcount * TILE, NRHS), "row", scatter_dimension=0, tiled=True)
-    own_forward = lax.psum_scatter(forward.reshape(groups * TILE, NRHS), "col", scatter_dimension=0, tiled=True)
-    return (own_forward + own_back).astype(jnp.bfloat16)
+    return scatter_sum(forward, backward, n_row, n_col)
 
 
 def solution(mesh):

time: 465 us -> 171 us (0.37)
  waiting for transfers between devices: 402 us -> 0 us
  Pallas kernels: 38.8 us -> 162 us
  between operations: 13.1 us -> 0.03 us
    reduce_scatter x2 -> x0, waiting for transfers between devices: 277 us -> none  [the longest x1 208 us: per_device(): lax.psum_scatter(backward.reshape(colcount * TILE, NRHS), 'row', scatter_...]
    all_gather x2 -> x0, waiting for transfers between devices: 124 us -> none  [the longest x1 88.1 us: per_device(): col_slab = lax.all_gather(panel_values, 'row', axis=0, tiled=True)]
    pallas_call x0 -> x2, Pallas kernels: none -> 123 us  [the longest x1 64.8 us: gather_slabs(): pl.pallas_call(functools.partial(gather_kernel, nr, nc), out_shape=[jax.S...]
  transfers between devices with their start and end apart: 4 -> 0, of which waited for: 4 -> 0; matrix products, arithmetic and copies ran while one was open for 0% -> 0% of each run, Pallas kernels for 0% -> 0%
where the time goes in v3:
time: 171 us; the launch traced here: 169 us
  Pallas kernels  162 us (95%)
  local copies, waits for them, and re-layouts  6.02 us (4%)
    pallas_call x1, Pallas kernels, gather_slabs(): pl.pallas_call(functools.partial(gather_kernel, nr, nc), out_shape=[jax.S...  64.8 us
    pallas_call x1, Pallas kernels, scatter_sum(): pl.pallas_call(functools.partial(scatter_kernel, nr, nc), out_shape=jax.S...  57.9 us
    pallas_call x1, Pallas kernels, local_products(): pl.pallas_call(local_kernel, grid_spec=grid_spec, out_shape=[jax.ShapeDty...  38.8 us
    unnamed x7, local copies, waits for them, and re-layouts  6.02 us

profile of v3, /device:TPU:2, one launch (start us, length us, event | category | flops | bytes accessed | tf_op | source)
XLA Modules:
  0.0 168.9 jit_solution(7667486992972660318)
XLA Ops:
  0.0 0.7 broadcast_subtract_fusion.1.near_idx
  0.7 0.7 broadcast_subtract_fusion.far_idx
  1.3 64.8 %shard_map.64 = (bf16[16,256,256]{2,1,0:T(8,128)(2,1)}, bf16[2,8,256,256]{3,2,1,0:T(8,128)(2,1)}) custom-call(bf16[256,256]{1,0:T(8,128)(2,1)} %x_ref.1), custom_call_target="tpu_custom_call" | custom-call | tf_op jit(solution)/shard_map/pallas_call | solution.py:151
  66.2 0.0 copy-start.1
  66.2 1.6 copy-done.1
  67.8 0.0 copy-start.2
  67.8 1.6 copy-done.2
  69.4 38.8 %shard_map.65 = (f32[16,256,256]{2,1,0:T(8,128)}, f32[16,256,256]{2,1,0:T(8,128)}) custom-call(s32[32]{0:T(128)S(1)} %broadcast_subtract_fusion.1.near_idx, s32[128]{0:T(128)S(1)} %broadcast_subtract_fusion.far_idx, bf16[32,256,256]{2,1,0:T(8,128)(2,1)} %tiles_ref.1, bf16[128,64,256]{2,1,0:T(8,128)(2,1)} %left_ref.1, bf16[128,64,256]{2,1,0:T(8,128)(2,1)} %right_ref.1, ...), custom_call_target="tpu_custom_call" | custom-call | flops 6442450944 | bytes 25165824 | tf_op jit(solution)/shard_map/pallas_call | solution.py:63
  108.2 0.0 copy-start
  108.2 2.2 %copy-done = f32[16,256,256]{2,1,0:T(8,128)S(1)} copy-done((f32[16,256,256]{2,1,0:T(8,128)S(1)}, f32[16,256,256]{2,1,0:T(8,128)}, u32[]{:S(2)}) %copy-start) | copy-done | bytes 4194328
  110.4 57.9 %shard_map.66 = bf16[256,256]{1,0:T(8,128)(2,1)S(1)} custom-call(f32[16,256,256]{2,1,0:T(8,128)S(1)} %copy-done, f32[2,8,256,256]{3,2,1,0:T(8,128)} %bitcast.3), custom_call_target="tpu_custom_call" | custom-call | tf_op jit(solution)/shard_map/pallas_call | solution.py:226
  168.2 0.7 copy.8
Async XLA Ops:
  66.2 1.6 copy-start.1
  67.8 1.6 copy-start.2
  108.2 2.2 %copy-start = (f32[16,256,256]{2,1,0:T(8,128)S(1)}, f32[16,256,256]{2,1,0:T(8,128)}, u32[]{:S(2)}) copy-start(f32[16,256,256]{2,1,0:T(8,128)} %get-tuple-element.11.f_ref) | copy-start | bytes 12582916

commit v4 on v3

--- a/solution.py
+++ b/solution.py
@@ -16,7 +16,8 @@
 TN = (((0,), (0,)), ((), ()))
 
 
-def local_kernel(near_idx, far_idx, tiles_ref, left_ref, right_ref, colx_ref, rowx_ref, f_ref, b_ref):
+def local_kernel(near_idx, far_idx, tiles_ref, left_ref, right_ref, colx_ref, rowx_ref, f_ref, b_ref,
+                 near_x, far_t):
     k = pl.program_id(0)
 
     @pl.when(k == 0)
@@ -24,20 +25,22 @@
         f_ref[...] = jnp.zeros_like(f_ref)
 
     xc = colx_ref[0]
-    acc = jnp.zeros((TILE, NRHS), jnp.float32)
+    tiles = tiles_ref[...].reshape(DPC * TILE, TILE)
+    near_f = jnp.dot(tiles, xc, preferred_element_type=jnp.float32)
     for d in range(DPC):
         r = near_idx[k * DPC + d]
-        t = tiles_ref[d]
-        f_ref[r] += jnp.dot(t, xc, preferred_element_type=jnp.float32)
-        acc += lax.dot_general(t, rowx_ref[r], TN, preferred_element_type=jnp.float32)
+        f_ref[r] += near_f[d * TILE:(d + 1) * TILE]
+        near_x[d * TILE:(d + 1) * TILE] = rowx_ref[r]
+    right = right_ref[...].reshape(LPC * RANK, TILE)
+    coef = jnp.dot(right, xc, preferred_element_type=jnp.float32).astype(jnp.bfloat16)
     for d in range(LPC):
         r = far_idx[k * LPC + d]
-        right = right_ref[d]
         left = left_ref[d]
-        coef = jnp.dot(right, xc, preferred_element_type=jnp.float32).astype(jnp.bfloat16)
-        f_ref[r] += lax.dot_general(left, coef, TN, preferred_element_type=jnp.float32)
-        tcoef = jnp.dot(left, rowx_ref[r], preferred_element_type=jnp.float32).astype(jnp.bfloat16)
-        acc += lax.dot_general(right, tcoef, TN, preferred_element_type=jnp.float32)
+        f_ref[r] += lax.dot_general(left, coef[d * RANK:(d + 1) * RANK], TN, preferred_element_type=jnp.float32)
+        far_t[d * RANK:(d + 1) * RANK] = jnp.dot(
+            left, rowx_ref[r], preferred_element_type=jnp.float32).astype(jnp.bfloat16)
+    acc = lax.dot_general(tiles, near_x[...], TN, preferred_element_type=jnp.float32)
+    acc += lax.dot_general(right, far_t[...], TN, preferred_element_type=jnp.float32)
     b_ref[0] = acc
 
 
@@ -57,6 +60,10 @@
         out_specs=[
             pl.BlockSpec((groups, TILE, NRHS), lambda k, a, b: (0, 0, 0)),
             pl.BlockSpec((1, TILE, NRHS), lambda k, a, b: (k, 0, 0)),
+        ],
+        scratch_shapes=[
+            pltpu.VMEM((DPC * TILE, NRHS), jnp.bfloat16),
+            pltpu.VMEM((LPC * RANK, NRHS), jnp.bfloat16),
         ],
     )
     flops = 2 * TILE * TILE * NRHS * near_tiles.shape[0] * 2 + 2 * RANK * TILE * NRHS * far_left.shape[0] * 4

time: 171 us -> 155 us (0.906)
  Pallas kernels: 162 us -> 145 us
    pallas_call x1, Pallas kernels: 38.8 us -> 22.4 us  [local_products(): pl.pallas_call(local_kernel, grid_spec=grid_spec, out_shape=[jax.ShapeDty...]
where the time goes in v4:
time: 155 us; the launch traced here: 152 us
  Pallas kernels  145 us (94%)
  local copies, waits for them, and re-layouts  6.02 us (4%)
    pallas_call x1, Pallas kernels, gather_slabs(): pl.pallas_call(functools.partial(gather_kernel, nr, nc), out_shape=[jax.S...  64.8 us
    pallas_call x1, Pallas kernels, scatter_sum(): pl.pallas_call(functools.partial(scatter_kernel, nr, nc), out_shape=jax.S...  57.9 us
    pallas_call x1, Pallas kernels, local_products(): pl.pallas_call(local_kernel, grid_spec=grid_spec, out_shape=[jax.ShapeDty...  22.4 us
    unnamed x7, local copies, waits for them, and re-layouts  6.02 us

profile of v4, /device:TPU:2, one launch (start us, length us, event | category | flops | bytes accessed | tf_op | source)
XLA Modules:
  0.0 152.5 jit_solution(14194175634096955366)
XLA Ops:
  0.0 0.7 broadcast_subtract_fusion.1.near_idx
  0.7 0.7 broadcast_subtract_fusion.far_idx
  1.3 64.8 %shard_map.64 = (bf16[16,256,256]{2,1,0:T(8,128)(2,1)}, bf16[2,8,256,256]{3,2,1,0:T(8,128)(2,1)}) custom-call(bf16[256,256]{1,0:T(8,128)(2,1)} %x_ref.1), custom_call_target="tpu_custom_call" | custom-call | tf_op jit(solution)/shard_map/pallas_call | solution.py:158
  66.2 0.0 copy-start.1
  66.2 1.6 %copy-done.1 = bf16[16,256,256]{2,1,0:T(8,128)(2,1)S(1)} copy-done((bf16[16,256,256]{2,1,0:T(8,128)(2,1)S(1)}, bf16[16,256,256]{2,1,0:T(8,128)(2,1)}, u32[]{:S(2)}) %copy-start.1) | copy-done | bytes 2097176
  67.8 0.0 copy-start.2
  67.8 1.6 %copy-done.2 = bf16[2,8,256,256]{3,2,1,0:T(8,128)(2,1)S(1)} copy-done((bf16[2,8,256,256]{3,2,1,0:T(8,128)(2,1)S(1)}, bf16[2,8,256,256]{3,2,1,0:T(8,128)(2,1)}, u32[]{:S(2)}) %copy-start.2) | copy-done | bytes 2097176
  69.4 22.4 %shard_map.65 = (f32[16,256,256]{2,1,0:T(8,128)}, f32[16,256,256]{2,1,0:T(8,128)}) custom-call(s32[32]{0:T(128)S(1)} %broadcast_subtract_fusion.1.near_idx, s32[128]{0:T(128)S(1)} %broadcast_subtract_fusion.far_idx, bf16[32,256,256]{2,1,0:T(8,128)(2,1)} %tiles_ref.1, bf16[128,64,256]{2,1,0:T(8,128)(2,1)} %left_ref.1, bf16[128,64,256]{2,1,0:T(8,128)(2,1)} %right_ref.1, ...), custom_call_target="tpu_custom_call" | custom-call | flops 6442450944 | bytes 25165824 | tf_op jit(solution)/shard_map/pallas_call | solution.py:70
  91.8 0.0 copy-start
  91.8 2.2 %copy-done = f32[16,256,256]{2,1,0:T(8,128)S(1)} copy-done((f32[16,256,256]{2,1,0:T(8,128)S(1)}, f32[16,256,256]{2,1,0:T(8,128)}, u32[]{:S(2)}) %copy-start) | copy-done | bytes 4194328
  94.0 57.9 %shard_map.66 = bf16[256,256]{1,0:T(8,128)(2,1)S(1)} custom-call(f32[16,256,256]{2,1,0:T(8,128)S(1)} %copy-done, f32[2,8,256,256]{3,2,1,0:T(8,128)} %bitcast.3), custom_call_target="tpu_custom_call" | custom-call | tf_op jit(solution)/shard_map/pallas_call | solution.py:233
  151.8 0.7 copy.8
Async XLA Ops:
  66.2 1.6 %copy-start.1 = (bf16[16,256,256]{2,1,0:T(8,128)(2,1)S(1)}, bf16[16,256,256]{2,1,0:T(8,128)(2,1)}, u32[]{:S(2)}) copy-start(bf16[16,256,256]{2,1,0:T(8,128)(2,1)} %get-tuple-element.10.rowx_ref) | copy-start | bytes 6291460
  67.8 1.6 %copy-start.2 = (bf16[2,8,256,256]{3,2,1,0:T(8,128)(2,1)S(1)}, bf16[2,8,256,256]{3,2,1,0:T(8,128)(2,1)}, u32[]{:S(2)}) copy-start(bf16[2,8,256,256]{3,2,1,0:T(8,128)(2,1)} %get-tuple-element.9) | copy-start | bytes 6291460
  91.8 2.2 %copy-start = (f32[16,256,256]{2,1,0:T(8,128)S(1)}, f32[16,256,256]{2,1,0:T(8,128)}, u32[]{:S(2)}) copy-start(f32[16,256,256]{2,1,0:T(8,128)} %get-tuple-element.11.f_ref) | copy-start | bytes 12582916

commit v5 on v4

--- a/solution.py
+++ b/solution.py
@@ -90,7 +90,11 @@
     half = nr // 2
     xh = i // half
     z = lax.rem(i, half)
-    cols = [(i, lax.rem(j + o, nc)) for o in range(1, nc)]
+    chips = nc // 2
+    core = lax.rem(j, 2)
+    chip = j // 2
+    cols = [(i, 2 * lax.rem(chip + o, chips) + core) for o in range(1, chips)]
+    cols.append((i, 2 * chip + 1 - core))
     right = (xh * half + lax.rem(z + 1, half), j)
     left = (xh * half + lax.rem(z + half - 1, half), j)
     partner = (lax.rem(i + half, nr), j)
@@ -113,6 +117,9 @@
     cw = half // 2
     ccw = half - 1 - cw
     enter(cols + [right, left, partner])
+    chips = nc // 2
+    core = lax.rem(j, 2)
+    chip = j // 2
     col_copies = [remote(x_ref, rowx_ref.at[j], col_send.at[n], col_recv.at[n], dev) for n, dev in enumerate(cols)]
     for c in col_copies:
         c.start()
@@ -147,8 +154,18 @@
         c.wait_send()
     prev_cw.wait_recv()
     prev_ccw.wait_recv()
-    for c in col_copies:
-        c.wait()
+    mate = cols[-1]
+    for o in range(1, chips):
+        origin = 2 * lax.rem(chip + chips - o, chips) + core
+        col_copies[o - 1].wait_recv()
+        c = remote(rowx_ref.at[origin], rowx_ref.at[origin], col_send.at[chips + o - 1],
+                   col_recv.at[chips + o - 1], mate)
+        c.start()
+        col_copies.append(c)
+    for c in col_copies:
+        c.wait_send()
+    for c in col_copies[chips - 1:]:
+        c.wait_recv()
     own_row.wait()
 
 
@@ -174,15 +191,18 @@
     )(x)
 
 
-def scatter_kernel(nr, nc, f_ref, b_ref, out_ref, recv_f, ring_in, ring_out, x_in, x_out,
+def scatter_kernel(nr, nc, f_ref, b_ref, out_ref, recv_f, pre, stage, ring_in, ring_out, x_in, x_out,
                    col_send, col_recv, ring_send, ring_recv, local_sem):
     i, j, half, xh, z, cols, right, left, partner = layout(nr, nc)
     cw = half // 2
     ccw = half - 1 - cw
     enter(cols + [right, left, partner])
-    col_copies = [
-        remote(f_ref.at[dev[1]], recv_f.at[n + 1], col_send.at[n], col_recv.at[n], dev) for n, dev in enumerate(cols)
-    ]
+    chips = nc // 2
+    core = lax.rem(j, 2)
+    chip = j // 2
+    mate = cols[-1]
+    handed = [2 * lax.rem(chip + o, chips) + 1 - core for o in range(1, chips)] + [mate[1]]
+    col_copies = [remote(f_ref.at[m], pre.at[n], col_send.at[n], col_recv.at[n], mate) for n, m in enumerate(handed)]
     for c in col_copies:
         c.start()
     sends = []
@@ -207,6 +227,14 @@
             c.start()
             sends.append(c)
             arrivals[(way, t)] = c
+    for c in col_copies:
+        c.wait_recv()
+    for o in range(1, chips):
+        dev = cols[o - 1]
+        stage[o - 1] = f_ref[dev[1]] + pre[o - 1]
+        c = remote(stage.at[o - 1], recv_f.at[o - 1], col_send.at[chips + o - 1], col_recv.at[chips + o - 1], dev)
+        c.start()
+        col_copies.append(c)
     arrivals[(0, cw)].wait_recv()
     arrivals[(1, ccw)].wait_recv()
     away = 1 - xh
@@ -216,10 +244,12 @@
     for c in sends:
         c.wait_send()
     for c in col_copies:
-        c.wait()
+        c.wait_send()
+    for c in col_copies[chips:]:
+        c.wait_recv()
     cross.wait()
-    acc = ring_in[cw - 1, xh] + ring_in[cw + ccw - 1, xh] + b_ref[xh, z] + x_in[...] + f_ref[j]
-    for n in range(1, nc):
+    acc = ring_in[cw - 1, xh] + ring_in[cw + ccw - 1, xh] + b_ref[xh, z] + x_in[...] + f_ref[j] + pre[chips - 1]
+    for n in range(chips - 1):
         acc = acc + recv_f[n]
     out_ref[...] = acc.astype(out_ref.dtype)
 
@@ -236,7 +266,9 @@
         in_specs=[pl.BlockSpec(memory_space=vmem)] * 2,
         out_specs=pl.BlockSpec(memory_space=vmem),
         scratch_shapes=[
-            vmem((nc,) + tile, jnp.float32),
+            vmem((nc // 2 - 1,) + tile, jnp.float32),
+            vmem((nc // 2,) + tile, jnp.float32),
+            vmem((nc // 2 - 1,) + tile, jnp.float32),
             vmem((steps, 2) + tile, jnp.float32),
             vmem((steps, 2) + tile, jnp.float32),
             vmem(tile, jnp.float32),

time: 155 us -> 157 us (1.013)
  Pallas kernels: 145 us -> 147 us
    pallas_call x1, Pallas kernels: 57.9 us -> 70.5 us  [scatter_sum(): pl.pallas_call(functools.partial(scatter_kernel, nr, nc), out_shape=jax.S...]
    pallas_call x1, Pallas kernels: 64.8 us -> 54.2 us  [gather_slabs(): pl.pallas_call(functools.partial(gather_kernel, nr, nc), out_shape=[jax.S...]
where the time goes in v5:
time: 157 us; the launch traced here: 155 us
  Pallas kernels  147 us (94%)
  local copies, waits for them, and re-layouts  6.02 us (4%)
    pallas_call x1, Pallas kernels, scatter_sum(): pl.pallas_call(functools.partial(scatter_kernel, nr, nc), out_shape=jax.S...  70.5 us
    pallas_call x1, Pallas kernels, gather_slabs(): pl.pallas_call(functools.partial(gather_kernel, nr, nc), out_shape=[jax.S...  54.2 us
    pallas_call x1, Pallas kernels, local_products(): pl.pallas_call(local_kernel, grid_spec=grid_spec, out_shape=[jax.ShapeDty...  22.4 us
    unnamed x7, local copies, waits for them, and re-layouts  6.02 us

profile of v5, /device:TPU:2, one launch (start us, length us, event | category | flops | bytes accessed | tf_op | source)
XLA Modules:
  0.0 154.5 jit_solution(749828689672555666)
XLA Ops:
  0.0 0.7 broadcast_subtract_fusion.1.near_idx
  0.7 0.7 broadcast_subtract_fusion.far_idx
  1.3 54.2 %shard_map.64 = (bf16[16,256,256]{2,1,0:T(8,128)(2,1)}, bf16[2,8,256,256]{3,2,1,0:T(8,128)(2,1)}) custom-call(bf16[256,256]{1,0:T(8,128)(2,1)} %x_ref.1), custom_call_target="tpu_custom_call" | custom-call | tf_op jit(solution)/shard_map/pallas_call | solution.py:175
  55.6 0.0 copy-start.1
  55.6 1.6 %copy-done.1 = bf16[16,256,256]{2,1,0:T(8,128)(2,1)S(1)} copy-done((bf16[16,256,256]{2,1,0:T(8,128)(2,1)S(1)}, bf16[16,256,256]{2,1,0:T(8,128)(2,1)}, u32[]{:S(2)}) %copy-start.1) | copy-done | bytes 2097176
  57.2 0.0 copy-start.2
  57.2 1.6 %copy-done.2 = bf16[2,8,256,256]{3,2,1,0:T(8,128)(2,1)S(1)} copy-done((bf16[2,8,256,256]{3,2,1,0:T(8,128)(2,1)S(1)}, bf16[2,8,256,256]{3,2,1,0:T(8,128)(2,1)}, u32[]{:S(2)}) %copy-start.2) | copy-done | bytes 2097176
  58.8 22.4 %shard_map.65 = (f32[16,256,256]{2,1,0:T(8,128)}, f32[16,256,256]{2,1,0:T(8,128)}) custom-call(s32[32]{0:T(128)S(1)} %broadcast_subtract_fusion.1.near_idx, s32[128]{0:T(128)S(1)} %broadcast_subtract_fusion.far_idx, bf16[32,256,256]{2,1,0:T(8,128)(2,1)} %tiles_ref.1, bf16[128,64,256]{2,1,0:T(8,128)(2,1)} %left_ref.1, bf16[128,64,256]{2,1,0:T(8,128)(2,1)} %right_ref.1, ...), custom_call_target="tpu_custom_call" | custom-call | flops 6442450944 | bytes 25165824 | tf_op jit(solution)/shard_map/pallas_call | solution.py:70
  81.2 0.0 copy-start
  81.2 2.2 %copy-done = f32[16,256,256]{2,1,0:T(8,128)S(1)} copy-done((f32[16,256,256]{2,1,0:T(8,128)S(1)}, f32[16,256,256]{2,1,0:T(8,128)}, u32[]{:S(2)}) %copy-start) | copy-done | bytes 4194328
  83.4 70.5 %shard_map.66 = bf16[256,256]{1,0:T(8,128)(2,1)S(1)} custom-call(f32[16,256,256]{2,1,0:T(8,128)S(1)} %copy-done, f32[2,8,256,256]{3,2,1,0:T(8,128)} %bitcast.3), custom_call_target="tpu_custom_call" | custom-call | tf_op jit(solution)/shard_map/pallas_call | solution.py:263
  153.9 0.7 copy.8
Async XLA Ops:
  55.6 1.6 %copy-start.1 = (bf16[16,256,256]{2,1,0:T(8,128)(2,1)S(1)}, bf16[16,256,256]{2,1,0:T(8,128)(2,1)}, u32[]{:S(2)}) copy-start(bf16[16,256,256]{2,1,0:T(8,128)(2,1)} %get-tuple-element.10.rowx_ref) | copy-start | bytes 6291460
  57.2 1.6 %copy-start.2 = (bf16[2,8,256,256]{3,2,1,0:T(8,128)(2,1)S(1)}, bf16[2,8,256,256]{3,2,1,0:T(8,128)(2,1)}, u32[]{:S(2)}) copy-start(bf16[2,8,256,256]{3,2,1,0:T(8,128)(2,1)} %get-tuple-element.9) | copy-start | bytes 6291460
  81.2 2.2 %copy-start = (f32[16,256,256]{2,1,0:T(8,128)S(1)}, f32[16,256,256]{2,1,0:T(8,128)}, u32[]{:S(2)}) copy-start(f32[16,256,256]{2,1,0:T(8,128)} %get-tuple-element.11.f_ref) | copy-start | bytes 12582916

commit v6 on v5

--- a/solution.py
+++ b/solution.py
@@ -129,39 +129,47 @@
     own_col = pltpu.make_async_copy(x_ref, colx_ref.at[xh, z], local_sem.at[1])
     own_row.start()
     own_col.start()
-    own_col.wait()
-    other.wait()
+    mate = cols[-1]
     ring = []
-    prev_cw = prev_ccw = None
-    for t in range(1, cw + 1):
-        origin = lax.rem(z - t + 1 + half, half)
-        if prev_cw is not None:
-            prev_cw.wait_recv()
-        c = remote(colx_ref.at[:, origin], colx_ref.at[:, origin], ring_send.at[t], ring_recv.at[t], right)
-        c.start()
-        ring.append(c)
-        prev_cw = c
-        if t <= ccw:
-            origin = lax.rem(z + t - 1, half)
-            if prev_ccw is not None:
-                prev_ccw.wait_recv()
-            c = remote(colx_ref.at[:, origin], colx_ref.at[:, origin], ring_send.at[cw + t],
-                       ring_recv.at[cw + t], left)
+    state = {}
+
+    def ring_step(t):
+        if t == 1:
+            own_col.wait()
+            other.wait()
+        for way in range(2):
+            if way == 1 and t > ccw:
+                continue
+            if way == 0:
+                origin = lax.rem(z - t + 1 + half, half)
+                sem, dev = t, right
+            else:
+                origin = lax.rem(z + t - 1, half)
+                sem, dev = cw + t, left
+            if t > 1:
+                state[way].wait_recv()
+            c = remote(colx_ref.at[:, origin], colx_ref.at[:, origin], ring_send.at[sem], ring_recv.at[sem], dev)
             c.start()
             ring.append(c)
-            prev_ccw = c
-    for c in ring:
-        c.wait_send()
-    prev_cw.wait_recv()
-    prev_ccw.wait_recv()
-    mate = cols[-1]
-    for o in range(1, chips):
+            state[way] = c
+
+    def col_step(o):
         origin = 2 * lax.rem(chip + chips - o, chips) + core
         col_copies[o - 1].wait_recv()
         c = remote(rowx_ref.at[origin], rowx_ref.at[origin], col_send.at[chips + o - 1],
                    col_recv.at[chips + o - 1], mate)
         c.start()
         col_copies.append(c)
+
+    for n in range(max(cw, chips - 1)):
+        if n < cw:
+            ring_step(n + 1)
+        if n < chips - 1:
+            col_step(n + 1)
+    for c in ring:
+        c.wait_send()
+    state[0].wait_recv()
+    state[1].wait_recv()
     for c in col_copies:
         c.wait_send()
     for c in col_copies[chips - 1:]:
@@ -207,7 +215,8 @@
         c.start()
     sends = []
     arrivals = {}
-    for t in range(1, cw + 1):
+
+    def ring_step(t):
         for way in range(2):
             if way == 1 and t > ccw:
                 continue
@@ -227,14 +236,21 @@
             c.start()
             sends.append(c)
             arrivals[(way, t)] = c
-    for c in col_copies:
-        c.wait_recv()
-    for o in range(1, chips):
+
+    def col_step(o):
         dev = cols[o - 1]
+        col_copies[o - 1].wait_recv()
         stage[o - 1] = f_ref[dev[1]] + pre[o - 1]
         c = remote(stage.at[o - 1], recv_f.at[o - 1], col_send.at[chips + o - 1], col_recv.at[chips + o - 1], dev)
         c.start()
         col_copies.append(c)
+
+    for n in range(max(cw, chips - 1)):
+        if n < cw:
+            ring_step(n + 1)
+        if n < chips - 1:
+            col_step(n + 1)
+    col_copies[chips - 1].wait_recv()
     arrivals[(0, cw)].wait_recv()
     arrivals[(1, ccw)].wait_recv()
     away = 1 - xh

time: 157 us -> 144 us (0.917)
  Pallas kernels: 147 us -> 134 us
    pallas_call x1, Pallas kernels: 70.5 us -> 59.8 us  [scatter_sum(): pl.pallas_call(functools.partial(scatter_kernel, nr, nc), out_shape=jax.S...]
    pallas_call x1, Pallas kernels: 54.2 us -> 51.8 us  [gather_slabs(): pl.pallas_call(functools.partial(gather_kernel, nr, nc), out_shape=[jax.S...]
where the time goes in v6:
time: 144 us; the launch traced here: 141 us
  Pallas kernels  134 us (93%)
  local copies, waits for them, and re-layouts  6.02 us (4%)
    pallas_call x1, Pallas kernels, scatter_sum(): pl.pallas_call(functools.partial(scatter_kernel, nr, nc), out_shape=jax.S...  59.8 us
    pallas_call x1, Pallas kernels, gather_slabs(): pl.pallas_call(functools.partial(gather_kernel, nr, nc), out_shape=[jax.S...  51.8 us
    pallas_call x1, Pallas kernels, local_products(): pl.pallas_call(local_kernel, grid_spec=grid_spec, out_shape=[jax.ShapeDty...  22.4 us
    unnamed x7, local copies, waits for them, and re-layouts  6.02 us

profile of v6, /device:TPU:2, one launch (start us, length us, event | category | flops | bytes accessed | tf_op | source)
XLA Modules:
  0.0 141.4 jit_solution(3311326614609254266)
XLA Ops:
  0.0 0.7 broadcast_subtract_fusion.1.near_idx
  0.7 0.7 broadcast_subtract_fusion.far_idx
  1.3 51.8 %shard_map.64 = (bf16[16,256,256]{2,1,0:T(8,128)(2,1)}, bf16[2,8,256,256]{3,2,1,0:T(8,128)(2,1)}) custom-call(bf16[256,256]{1,0:T(8,128)(2,1)} %x_ref.1), custom_call_target="tpu_custom_call" | custom-call | tf_op jit(solution)/shard_map/pallas_call | solution.py:183
  53.1 0.0 copy-start.1
  53.2 1.6 %copy-done.1 = bf16[16,256,256]{2,1,0:T(8,128)(2,1)S(1)} copy-done((bf16[16,256,256]{2,1,0:T(8,128)(2,1)S(1)}, bf16[16,256,256]{2,1,0:T(8,128)(2,1)}, u32[]{:S(2)}) %copy-start.1) | copy-done | bytes 2097176
  54.7 0.0 copy-start.2
  54.7 1.6 %copy-done.2 = bf16[2,8,256,256]{3,2,1,0:T(8,128)(2,1)S(1)} copy-done((bf16[2,8,256,256]{3,2,1,0:T(8,128)(2,1)S(1)}, bf16[2,8,256,256]{3,2,1,0:T(8,128)(2,1)}, u32[]{:S(2)}) %copy-start.2) | copy-done | bytes 2097176
  56.3 22.4 %shard_map.65 = (f32[16,256,256]{2,1,0:T(8,128)}, f32[16,256,256]{2,1,0:T(8,128)}) custom-call(s32[32]{0:T(128)S(1)} %broadcast_subtract_fusion.1.near_idx, s32[128]{0:T(128)S(1)} %broadcast_subtract_fusion.far_idx, bf16[32,256,256]{2,1,0:T(8,128)(2,1)} %tiles_ref.1, bf16[128,64,256]{2,1,0:T(8,128)(2,1)} %left_ref.1, bf16[128,64,256]{2,1,0:T(8,128)(2,1)} %right_ref.1, ...), custom_call_target="tpu_custom_call" | custom-call | flops 6442450944 | bytes 25165824 | tf_op jit(solution)/shard_map/pallas_call | solution.py:70
  78.8 0.0 copy-start
  78.8 2.2 %copy-done = f32[16,256,256]{2,1,0:T(8,128)S(1)} copy-done((f32[16,256,256]{2,1,0:T(8,128)S(1)}, f32[16,256,256]{2,1,0:T(8,128)}, u32[]{:S(2)}) %copy-start) | copy-done | bytes 4194328
  81.0 59.8 %shard_map.66 = bf16[256,256]{1,0:T(8,128)(2,1)S(1)} custom-call(f32[16,256,256]{2,1,0:T(8,128)S(1)} %copy-done, f32[2,8,256,256]{3,2,1,0:T(8,128)} %bitcast.3), custom_call_target="tpu_custom_call" | custom-call | tf_op jit(solution)/shard_map/pallas_call | solution.py:279
  140.7 0.7 copy.8
Async XLA Ops:
  53.1 1.6 %copy-start.1 = (bf16[16,256,256]{2,1,0:T(8,128)(2,1)S(1)}, bf16[16,256,256]{2,1,0:T(8,128)(2,1)}, u32[]{:S(2)}) copy-start(bf16[16,256,256]{2,1,0:T(8,128)(2,1)} %get-tuple-element.10.rowx_ref) | copy-start | bytes 6291460
  54.7 1.6 %copy-start.2 = (bf16[2,8,256,256]{3,2,1,0:T(8,128)(2,1)S(1)}, bf16[2,8,256,256]{3,2,1,0:T(8,128)(2,1)}, u32[]{:S(2)}) copy-start(bf16[2,8,256,256]{3,2,1,0:T(8,128)(2,1)} %get-tuple-element.9) | copy-start | bytes 6291460
  78.8 2.2 %copy-start = (f32[16,256,256]{2,1,0:T(8,128)S(1)}, f32[16,256,256]{2,1,0:T(8,128)}, u32[]{:S(2)}) copy-start(f32[16,256,256]{2,1,0:T(8,128)} %get-tuple-element.11.f_ref) | copy-start | bytes 12582916

commit v7 on v6

--- a/solution.py
+++ b/solution.py
@@ -16,37 +16,38 @@
 TN = (((0,), (0,)), ((), ()))
 
 
-def local_kernel(near_idx, far_idx, tiles_ref, left_ref, right_ref, colx_ref, rowx_ref, f_ref, b_ref,
-                 near_x, far_t):
+def local_kernel(half, near_idx, far_idx, tiles_ref, left_ref, right_ref, slab_ref, out_ref, near_x, far_t):
     k = pl.program_id(0)
+    base = slab_ref.shape[0] - 2
+    fb = out_ref.shape[0] - 2
 
     @pl.when(k == 0)
     def _():
-        f_ref[...] = jnp.zeros_like(f_ref)
-
-    xc = colx_ref[0]
+        out_ref[0:fb] = jnp.zeros(out_ref.shape[1:], jnp.float32)[None].repeat(fb, 0)
+
+    xc = slab_ref[base + k // half, lax.rem(k, half)]
     tiles = tiles_ref[...].reshape(DPC * TILE, TILE)
     near_f = jnp.dot(tiles, xc, preferred_element_type=jnp.float32)
     for d in range(DPC):
         r = near_idx[k * DPC + d]
-        f_ref[r] += near_f[d * TILE:(d + 1) * TILE]
-        near_x[d * TILE:(d + 1) * TILE] = rowx_ref[r]
+        out_ref[r // half, lax.rem(r, half)] += near_f[d * TILE:(d + 1) * TILE]
+        near_x[d * TILE:(d + 1) * TILE] = slab_ref[r // half, lax.rem(r, half)]
     right = right_ref[...].reshape(LPC * RANK, TILE)
     coef = jnp.dot(right, xc, preferred_element_type=jnp.float32).astype(jnp.bfloat16)
     for d in range(LPC):
         r = far_idx[k * LPC + d]
         left = left_ref[d]
-        f_ref[r] += lax.dot_general(left, coef[d * RANK:(d + 1) * RANK], TN, preferred_element_type=jnp.float32)
+        out_ref[r // half, lax.rem(r, half)] += lax.dot_general(
+            left, coef[d * RANK:(d + 1) * RANK], TN, preferred_element_type=jnp.float32)
         far_t[d * RANK:(d + 1) * RANK] = jnp.dot(
-            left, rowx_ref[r], preferred_element_type=jnp.float32).astype(jnp.bfloat16)
+            left, slab_ref[r // half, lax.rem(r, half)], preferred_element_type=jnp.float32).astype(jnp.bfloat16)
     acc = lax.dot_general(tiles, near_x[...], TN, preferred_element_type=jnp.float32)
     acc += lax.dot_general(right, far_t[...], TN, preferred_element_type=jnp.float32)
-    b_ref[0] = acc
-
-
-def local_products(near_local, far_local, near_tiles, far_left, far_right, colx, rowx):
-    count = colx.shape[0]
-    groups = rowx.shape[0]
+    out_ref[fb + k // half, lax.rem(k, half)] = acc
+
+
+def local_products(near_local, far_local, near_tiles, far_left, far_right, slab, count, groups):
+    half = slab.shape[1]
     grid_spec = pltpu.PrefetchScalarGridSpec(
         num_scalar_prefetch=2,
         grid=(count,),
@@ -54,13 +55,9 @@
             pl.BlockSpec((DPC, TILE, TILE), lambda k, a, b: (k, 0, 0)),
             pl.BlockSpec((LPC, RANK, TILE), lambda k, a, b: (k, 0, 0)),
             pl.BlockSpec((LPC, RANK, TILE), lambda k, a, b: (k, 0, 0)),
-            pl.BlockSpec((1, TILE, NRHS), lambda k, a, b: (k, 0, 0)),
-            pl.BlockSpec((groups, TILE, NRHS), lambda k, a, b: (0, 0, 0)),
+            pl.BlockSpec(memory_space=pltpu.VMEM),
         ],
-        out_specs=[
-            pl.BlockSpec((groups, TILE, NRHS), lambda k, a, b: (0, 0, 0)),
-            pl.BlockSpec((1, TILE, NRHS), lambda k, a, b: (k, 0, 0)),
-        ],
+        out_specs=pl.BlockSpec(memory_space=pltpu.VMEM),
         scratch_shapes=[
             pltpu.VMEM((DPC * TILE, NRHS), jnp.bfloat16),
             pltpu.VMEM((LPC * RANK, NRHS), jnp.bfloat16),
@@ -68,17 +65,14 @@
     )
     flops = 2 * TILE * TILE * NRHS * near_tiles.shape[0] * 2 + 2 * RANK * TILE * NRHS * far_left.shape[0] * 4
     return pl.pallas_call(
-        local_kernel,
+        functools.partial(local_kernel, half),
         grid_spec=grid_spec,
-        out_shape=[
-            jax.ShapeDtypeStruct((groups, TILE, NRHS), jnp.float32),
-            jax.ShapeDtypeStruct((count, TILE, NRHS), jnp.float32),
-        ],
+        out_shape=jax.ShapeDtypeStruct((groups // half + 2, half, TILE, NRHS), jnp.float32),
         compiler_params=pltpu.CompilerParams(
             dimension_semantics=("arbitrary",), vmem_limit_bytes=48 * 1024 * 1024
         ),
         cost_estimate=pl.CostEstimate(flops=flops, bytes_accessed=24 * 1024 * 1024, transcendentals=0),
-    )(near_local, far_local, near_tiles, far_left, far_right, colx, rowx)
+    )(near_local, far_local, near_tiles, far_left, far_right, slab)
 
 
 MESH_ID = pl.DeviceIdType.MESH
@@ -112,7 +106,7 @@
     return pltpu.make_async_remote_copy(src, dst, ssem, rsem, device_id=dev, device_id_type=MESH_ID)
 
 
-def gather_kernel(nr, nc, x_ref, rowx_ref, colx_ref, col_send, col_recv, ring_send, ring_recv, local_sem):
+def gather_kernel(nr, nc, x_ref, slab_ref, col_send, col_recv, ring_send, ring_recv, local_sem):
     i, j, half, xh, z, cols, right, left, partner = layout(nr, nc)
     cw = half // 2
     ccw = half - 1 - cw
@@ -120,13 +114,15 @@
     chips = nc // 2
     core = lax.rem(j, 2)
     chip = j // 2
-    col_copies = [remote(x_ref, rowx_ref.at[j], col_send.at[n], col_recv.at[n], dev) for n, dev in enumerate(cols)]
+    base = nc // half
+    mine = slab_ref.at[j // half, lax.rem(j, half)]
+    col_copies = [remote(x_ref, mine, col_send.at[n], col_recv.at[n], dev) for n, dev in enumerate(cols)]
     for c in col_copies:
         c.start()
-    other = remote(x_ref, colx_ref.at[xh, z], ring_send.at[0], ring_recv.at[0], partner)
+    other = remote(x_ref, slab_ref.at[base + xh, z], ring_send.at[0], ring_recv.at[0], partner)
     other.start()
-    own_row = pltpu.make_async_copy(x_ref, rowx_ref.at[j], local_sem.at[0])
-    own_col = pltpu.make_async_copy(x_ref, colx_ref.at[xh, z], local_sem.at[1])
+    own_row = pltpu.make_async_copy(x_ref, mine, local_sem.at[0])
+    own_col = pltpu.make_async_copy(x_ref, slab_ref.at[base + xh, z], local_sem.at[1])
     own_row.start()
     own_col.start()
     mate = cols[-1]
@@ -148,7 +144,7 @@
                 sem, dev = cw + t, left
             if t > 1:
                 state[way].wait_recv()
-            c = remote(colx_ref.at[:, origin], colx_ref.at[:, origin], ring_send.at[sem], ring_recv.at[sem], dev)
+            c = remote(slab_ref.at[base:base + 2, origin], slab_ref.at[base:base + 2, origin], ring_send.at[sem], ring_recv.at[sem], dev)
             c.start()
             ring.append(c)
             state[way] = c
@@ -156,7 +152,7 @@
     def col_step(o):
         origin = 2 * lax.rem(chip + chips - o, chips) + core
         col_copies[o - 1].wait_recv()
-        c = remote(rowx_ref.at[origin], rowx_ref.at[origin], col_send.at[chips + o - 1],
+        c = remote(slab_ref.at[origin // half, lax.rem(origin, half)], slab_ref.at[origin // half, lax.rem(origin, half)], col_send.at[chips + o - 1],
                    col_recv.at[chips + o - 1], mate)
         c.start()
         col_copies.append(c)
@@ -182,12 +178,9 @@
     half = nr // 2
     return pl.pallas_call(
         functools.partial(gather_kernel, nr, nc),
-        out_shape=[
-            jax.ShapeDtypeStruct((nc,) + tile, x.dtype),
-            jax.ShapeDtypeStruct((2, half) + tile, x.dtype),
-        ],
+        out_shape=jax.ShapeDtypeStruct((nc // half + 2, half) + tile, x.dtype),
         in_specs=[pl.BlockSpec(memory_space=pl.ANY)],
-        out_specs=[pl.BlockSpec(memory_space=pl.ANY)] * 2,
+        out_specs=pl.BlockSpec(memory_space=pltpu.VMEM),
         scratch_shapes=[
             pltpu.SemaphoreType.DMA((nc - 1,)),
             pltpu.SemaphoreType.DMA((nc - 1,)),
@@ -199,7 +192,7 @@
     )(x)
 
 
-def scatter_kernel(nr, nc, f_ref, b_ref, out_ref, recv_f, pre, stage, ring_in, ring_out, x_in, x_out,
+def scatter_kernel(nr, nc, p_ref, out_ref, recv_f, pre, stage, ring_in, ring_out, x_in, x_out,
                    col_send, col_recv, ring_send, ring_recv, local_sem):
     i, j, half, xh, z, cols, right, left, partner = layout(nr, nc)
     cw = half // 2
@@ -208,9 +201,10 @@
     chips = nc // 2
     core = lax.rem(j, 2)
     chip = j // 2
+    fb = nc // half
     mate = cols[-1]
     handed = [2 * lax.rem(chip + o, chips) + 1 - core for o in range(1, chips)] + [mate[1]]
-    col_copies = [remote(f_ref.at[m], pre.at[n], col_send.at[n], col_recv.at[n], mate) for n, m in enumerate(handed)]
+    col_copies = [remote(p_ref.at[m // half, lax.rem(m, half)], pre.at[n], col_send.at[n], col_recv.at[n], mate) for n, m in enumerate(handed)]
     for c in col_copies:
         c.start()
     sends = []
@@ -227,10 +221,10 @@
                 target = lax.rem(z + half - (ccw + 1 - t), half)
                 slot, dev = cw + t - 1, left
             if t == 1:
-                src = b_ref.at[:, target]
+                src = p_ref.at[fb:fb + 2, target]
             else:
                 arrivals[(way, t - 1)].wait_recv()
-                ring_out[slot] = ring_in[slot - 1] + b_ref[:, target]
+                ring_out[slot] = ring_in[slot - 1] + p_ref[fb:fb + 2, target]
                 src = ring_out.at[slot]
             c = remote(src, ring_in.at[slot], ring_send.at[slot], ring_recv.at[slot], dev)
             c.start()
@@ -240,7 +234,7 @@
     def col_step(o):
         dev = cols[o - 1]
         col_copies[o - 1].wait_recv()
-        stage[o - 1] = f_ref[dev[1]] + pre[o - 1]
+        stage[o - 1] = p_ref[dev[1] // half, lax.rem(dev[1], half)] + pre[o - 1]
         c = remote(stage.at[o - 1], recv_f.at[o - 1], col_send.at[chips + o - 1], col_recv.at[chips + o - 1], dev)
         c.start()
         col_copies.append(c)
@@ -254,7 +248,7 @@
     arrivals[(0, cw)].wait_recv()
     arrivals[(1, ccw)].wait_recv()
     away = 1 - xh
-    x_out[...] = ring_in[cw - 1, away] + ring_in[cw + ccw - 1, away] + b_ref[away, z]
+    x_out[...] = ring_in[cw - 1, away] + ring_in[cw + ccw - 1, away] + p_ref[fb + away, z]
     cross = remote(x_out, x_in, ring_send.at[half - 1], ring_recv.at[half - 1], partner)
     cross.start()
     for c in sends:
@@ -264,14 +258,14 @@
     for c in col_copies[chips:]:
         c.wait_recv()
     cross.wait()
-    acc = ring_in[cw - 1, xh] + ring_in[cw + ccw - 1, xh] + b_ref[xh, z] + x_in[...] + f_ref[j] + pre[chips - 1]
+    acc = ring_in[cw - 1, xh] + ring_in[cw + ccw - 1, xh] + p_ref[fb + xh, z] + x_in[...] + p_ref[j // half, lax.rem(j, half)] + pre[chips - 1]
     for n in range(chips - 1):
         acc = acc + recv_f[n]
     out_ref[...] = acc.astype(out_ref.dtype)
 
 
-def scatter_sum(forward, backward, nr, nc):
-    tile = forward.shape[1:]
+def scatter_sum(partial, nr, nc):
+    tile = partial.shape[2:]
     half = nr // 2
     cw = half // 2
     steps = half - 1
@@ -279,7 +273,7 @@
     return pl.pallas_call(
         functools.partial(scatter_kernel, nr, nc),
         out_shape=jax.ShapeDtypeStruct(tile, jnp.bfloat16),
-        in_specs=[pl.BlockSpec(memory_space=vmem)] * 2,
+        in_specs=[pl.BlockSpec(memory_space=vmem)],
         out_specs=pl.BlockSpec(memory_space=vmem),
         scratch_shapes=[
             vmem((nc // 2 - 1,) + tile, jnp.float32),
@@ -297,7 +291,7 @@
         ],
         compiler_params=pltpu.CompilerParams(
             collective_id=1, has_side_effects=True, vmem_limit_bytes=48 * 1024 * 1024),
-    )(forward, backward.reshape((2, half) + tile))
+    )(partial)
 
 
 def per_device(panel_values, near_tiles, far_left, far_right, near_rows, far_rows):
@@ -309,10 +303,9 @@
     row_base = lax.axis_index("row") * groups
     near_local = near_rows - row_base
     far_local = far_rows - row_base
-    rowx, colx = gather_slabs(panel_values, n_row, n_col)
-    colx = colx.reshape(colcount, TILE, NRHS)
-    forward, backward = local_products(near_local, far_local, near_tiles, far_left, far_right, colx, rowx)
-    return scatter_sum(forward, backward, n_row, n_col)
+    slab = gather_slabs(panel_values, n_row, n_col)
+    partial = local_products(near_local, far_local, near_tiles, far_left, far_right, slab, colcount, groups)
+    return scatter_sum(partial, n_row, n_col)
 
 
 def solution(mesh):

time: 144 us -> 146 us (1.014)
  the two profiles are of different devices: /device:TPU:2 before, /device:TPU:18 now
where the time goes in v7:
time: 146 us
  Pallas kernels  142 us (97%)
  local copies, waits for them, and re-layouts  2.84 us (2%)
    pallas_call x1, Pallas kernels, scatter_sum(): pl.pallas_call(functools.partial(scatter_kernel, nr, nc), out_shape=jax.S...  66.6 us
    pallas_call x1, Pallas kernels, gather_slabs(): pl.pallas_call(functools.partial(gather_kernel, nr, nc), out_shape=jax.Sh...  50 us
    pallas_call x1, Pallas kernels, local_products(): pl.pallas_call(functools.partial(local_kernel, half), grid_spec=grid_spec...  25 us

profile of v7, /device:TPU:18, one launch (start us, length us, event | category | flops | bytes accessed | tf_op | source)
XLA Modules:
  0.0 145.8 jit_solution(2602454008778071640)
XLA Ops:
  0.0 0.7 broadcast_subtract_fusion.1.near_idx
  0.7 0.7 broadcast_subtract_fusion.far_idx
  1.3 50.0 %shard_map.64.slab_ref = bf16[4,8,256,256]{3,2,1,0:T(8,128)(2,1)} custom-call(bf16[256,256]{1,0:T(8,128)(2,1)} %x_ref.1), custom_call_target="tpu_custom_call" | custom-call | tf_op jit(solution)/shard_map/pallas_call | solution.py:179
  51.3 0.0 copy-start
  51.4 2.2 %copy-done = bf16[32,256,256]{2,1,0:T(8,128)(2,1)S(1)} copy-done((bf16[32,256,256]{2,1,0:T(8,128)(2,1)S(1)}, bf16[32,256,256]{2,1,0:T(8,128)(2,1)}, u32[]{:S(2)}) %copy-start) | copy-done | bytes 4194328
  53.5 25.0 %shard_map.65.p_ref = f32[4,8,256,256]{3,2,1,0:T(8,128)} custom-call(s32[32]{0:T(128)S(1)} %broadcast_subtract_fusion.1.near_idx, s32[128]{0:T(128)S(1)} %broadcast_subtract_fusion.far_idx, bf16[32,256,256]{2,1,0:T(8,128)(2,1)S(1)} %copy-done, bf16[128,64,256]{2,1,0:T(8,128)(2,1)} %left_ref.1, bf16[128,64,256]{2,1,0:T(8,128)(2,1)} %right_ref.1, ...), custom_call_target="tpu_custom_call" | custom-call | flops 6442450944 | bytes 25165824 | tf_op jit(solution)/shard_map/pallas_call | solution.py:67
  78.5 66.6 %shard_map.66 = bf16[256,256]{1,0:T(8,128)(2,1)S(1)} custom-call(f32[4,8,256,256]{3,2,1,0:T(8,128)} %shard_map.65.p_ref), custom_call_target="tpu_custom_call" | custom-call | tf_op jit(solution)/shard_map/pallas_call | solution.py:273
  145.1 0.7 copy.8
Async XLA Ops:
  51.3 2.2 %copy-start = (bf16[32,256,256]{2,1,0:T(8,128)(2,1)S(1)}, bf16[32,256,256]{2,1,0:T(8,128)(2,1)}, u32[]{:S(2)}) copy-start(bf16[32,256,256]{2,1,0:T(8,128)(2,1)} %tiles_ref.1) | copy-start | bytes 12582916

commit v8 on v7

--- a/solution.py
+++ b/solution.py
@@ -16,14 +16,13 @@
 TN = (((0,), (0,)), ((), ()))
 
 
-def local_kernel(half, near_idx, far_idx, tiles_ref, left_ref, right_ref, slab_ref, out_ref, near_x, far_t):
+def local_kernel(half, near_idx, far_idx, tiles_ref, left_ref, right_ref, slab_ref, out_ref):
     k = pl.program_id(0)
     base = slab_ref.shape[0] - 2
-    fb = out_ref.shape[0] - 2
 
     @pl.when(k == 0)
     def _():
-        out_ref[0:fb] = jnp.zeros(out_ref.shape[1:], jnp.float32)[None].repeat(fb, 0)
+        out_ref[...] = jnp.zeros_like(out_ref)
 
     xc = slab_ref[base + k // half, lax.rem(k, half)]
     tiles = tiles_ref[...].reshape(DPC * TILE, TILE)
@@ -31,19 +30,12 @@
     for d in range(DPC):
         r = near_idx[k * DPC + d]
         out_ref[r // half, lax.rem(r, half)] += near_f[d * TILE:(d + 1) * TILE]
-        near_x[d * TILE:(d + 1) * TILE] = slab_ref[r // half, lax.rem(r, half)]
     right = right_ref[...].reshape(LPC * RANK, TILE)
     coef = jnp.dot(right, xc, preferred_element_type=jnp.float32).astype(jnp.bfloat16)
     for d in range(LPC):
         r = far_idx[k * LPC + d]
-        left = left_ref[d]
         out_ref[r // half, lax.rem(r, half)] += lax.dot_general(
-            left, coef[d * RANK:(d + 1) * RANK], TN, preferred_element_type=jnp.float32)
-        far_t[d * RANK:(d + 1) * RANK] = jnp.dot(
-            left, slab_ref[r // half, lax.rem(r, half)], preferred_element_type=jnp.float32).astype(jnp.bfloat16)
-    acc = lax.dot_general(tiles, near_x[...], TN, preferred_element_type=jnp.float32)
-    acc += lax.dot_general(right, far_t[...], TN, preferred_element_type=jnp.float32)
-    out_ref[fb + k // half, lax.rem(k, half)] = acc
+            left_ref[d], coef[d * RANK:(d + 1) * RANK], TN, preferred_element_type=jnp.float32)
 
 
 def local_products(near_local, far_local, near_tiles, far_left, far_right, slab, count, groups):
@@ -58,20 +50,16 @@
             pl.BlockSpec(memory_space=pltpu.VMEM),
         ],
         out_specs=pl.BlockSpec(memory_space=pltpu.VMEM),
-        scratch_shapes=[
-            pltpu.VMEM((DPC * TILE, NRHS), jnp.bfloat16),
-            pltpu.VMEM((LPC * RANK, NRHS), jnp.bfloat16),
-        ],
     )
-    flops = 2 * TILE * TILE * NRHS * near_tiles.shape[0] * 2 + 2 * RANK * TILE * NRHS * far_left.shape[0] * 4
+    flops = 2 * TILE * TILE * NRHS * near_tiles.shape[0] + 2 * RANK * TILE * NRHS * far_left.shape[0] * 2
     return pl.pallas_call(
         functools.partial(local_kernel, half),
         grid_spec=grid_spec,
-        out_shape=jax.ShapeDtypeStruct((groups // half + 2, half, TILE, NRHS), jnp.float32),
+        out_shape=jax.ShapeDtypeStruct((groups // half, half, TILE, NRHS), jnp.float32),
         compiler_params=pltpu.CompilerParams(
             dimension_semantics=("arbitrary",), vmem_limit_bytes=48 * 1024 * 1024
         ),
-        cost_estimate=pl.CostEstimate(flops=flops, bytes_accessed=24 * 1024 * 1024, transcendentals=0),
+        cost_estimate=pl.CostEstimate(flops=flops, bytes_accessed=16 * 1024 * 1024, transcendentals=0),
     )(near_local, far_local, near_tiles, far_left, far_right, slab)
 
 
@@ -192,16 +180,20 @@
     )(x)
 
 
-def scatter_kernel(nr, nc, p_ref, out_ref, recv_f, pre, stage, ring_in, ring_out, x_in, x_out,
+def scatter_kernel(nr, nc, near_idx, far_idx, p_ref, slab_ref, tiles_hbm, left_hbm, right_hbm, out_ref,
+                   tiles_v, left_v, right_v, b_buf, near_x, far_t, recv_f, pre, stage, ring_in, ring_out, x_in, x_out,
                    col_send, col_recv, ring_send, ring_recv, local_sem):
     i, j, half, xh, z, cols, right, left, partner = layout(nr, nc)
     cw = half // 2
     ccw = half - 1 - cw
+    loads = [pltpu.make_async_copy(src, dst, local_sem.at[n])
+             for n, (src, dst) in enumerate([(tiles_hbm, tiles_v), (right_hbm, right_v), (left_hbm, left_v)])]
+    for c in loads:
+        c.start()
     enter(cols + [right, left, partner])
     chips = nc // 2
     core = lax.rem(j, 2)
     chip = j // 2
-    fb = nc // half
     mate = cols[-1]
     handed = [2 * lax.rem(chip + o, chips) + 1 - core for o in range(1, chips)] + [mate[1]]
     col_copies = [remote(p_ref.at[m // half, lax.rem(m, half)], pre.at[n], col_send.at[n], col_recv.at[n], mate) for n, m in enumerate(handed)]
@@ -209,6 +201,22 @@
         c.start()
     sends = []
     arrivals = {}
+    for c in loads:
+        c.wait()
+
+    def back(xhp, target):
+        k = xhp * half + target
+        tiles = tiles_v[pl.ds(k * DPC, DPC)].reshape(DPC * TILE, TILE)
+        for d in range(DPC):
+            near_x[d * TILE:(d + 1) * TILE] = slab_ref[near_idx[k * DPC + d]]
+        rfac = right_v[pl.ds(k * LPC, LPC)].reshape(LPC * RANK, TILE)
+        for d in range(LPC):
+            far_t[d * RANK:(d + 1) * RANK] = jnp.dot(
+                left_v[k * LPC + d], slab_ref[far_idx[k * LPC + d]], preferred_element_type=jnp.float32
+            ).astype(jnp.bfloat16)
+        acc = lax.dot_general(tiles, near_x[...], TN, preferred_element_type=jnp.float32)
+        acc += lax.dot_general(rfac, far_t[...], TN, preferred_element_type=jnp.float32)
+        b_buf[xhp, target] = acc
 
     def ring_step(t):
         for way in range(2):
@@ -220,11 +228,13 @@
             else:
                 target = lax.rem(z + half - (ccw + 1 - t), half)
                 slot, dev = cw + t - 1, left
+            back(0, target)
+            back(1, target)
             if t == 1:
-                src = p_ref.at[fb:fb + 2, target]
+                src = b_buf.at[:, target]
             else:
                 arrivals[(way, t - 1)].wait_recv()
-                ring_out[slot] = ring_in[slot - 1] + p_ref[fb:fb + 2, target]
+                ring_out[slot] = ring_in[slot - 1] + b_buf[:, target]
                 src = ring_out.at[slot]
             c = remote(src, ring_in.at[slot], ring_send.at[slot], ring_recv.at[slot], dev)
             c.start()
@@ -244,11 +254,13 @@
             ring_step(n + 1)
         if n < chips - 1:
             col_step(n + 1)
+    back(0, z)
+    back(1, z)
     col_copies[chips - 1].wait_recv()
     arrivals[(0, cw)].wait_recv()
     arrivals[(1, ccw)].wait_recv()
     away = 1 - xh
-    x_out[...] = ring_in[cw - 1, away] + ring_in[cw + ccw - 1, away] + p_ref[fb + away, z]
+    x_out[...] = ring_in[cw - 1, away] + ring_in[cw + ccw - 1, away] + b_buf[away, z]
     cross = remote(x_out, x_in, ring_send.at[half - 1], ring_recv.at[half - 1], partner)
     cross.start()
     for c in sends:
@@ -258,13 +270,13 @@
     for c in col_copies[chips:]:
         c.wait_recv()
     cross.wait()
-    acc = ring_in[cw - 1, xh] + ring_in[cw + ccw - 1, xh] + p_ref[fb + xh, z] + x_in[...] + p_ref[j // half, lax.rem(j, half)] + pre[chips - 1]
+    acc = ring_in[cw - 1, xh] + ring_in[cw + ccw - 1, xh] + b_buf[xh, z] + x_in[...] + p_ref[j // half, lax.rem(j, half)] + pre[chips - 1]
     for n in range(chips - 1):
         acc = acc + recv_f[n]
     out_ref[...] = acc.astype(out_ref.dtype)
 
 
-def scatter_sum(partial, nr, nc):
+def scatter_sum(partial, slab, near_local, far_local, near_tiles, far_left, far_right, nr, nc):
     tile = partial.shape[2:]
     half = nr // 2
     cw = half // 2
@@ -273,9 +285,17 @@
     return pl.pallas_call(
         functools.partial(scatter_kernel, nr, nc),
         out_shape=jax.ShapeDtypeStruct(tile, jnp.bfloat16),
-        in_specs=[pl.BlockSpec(memory_space=vmem)],
+        in_specs=[pl.BlockSpec(memory_space=pltpu.SMEM)] * 2
+        + [pl.BlockSpec(memory_space=vmem)] * 2
+        + [pl.BlockSpec(memory_space=pl.ANY)] * 3,
         out_specs=pl.BlockSpec(memory_space=vmem),
         scratch_shapes=[
+            vmem(near_tiles.shape, near_tiles.dtype),
+            vmem(far_left.shape, far_left.dtype),
+            vmem(far_right.shape, far_right.dtype),
+            vmem((2, half) + tile, jnp.float32),
+            vmem((DPC * TILE, NRHS), jnp.bfloat16),
+            vmem((LPC * RANK, NRHS), jnp.bfloat16),
             vmem((nc // 2 - 1,) + tile, jnp.float32),
             vmem((nc // 2,) + tile, jnp.float32),
             vmem((nc // 2 - 1,) + tile, jnp.float32),
@@ -287,11 +307,11 @@
             pltpu.SemaphoreType.DMA((nc - 1,)),
             pltpu.SemaphoreType.DMA((half,)),
             pltpu.SemaphoreType.DMA((half,)),
-            pltpu.SemaphoreType.DMA((2,)),
+            pltpu.SemaphoreType.DMA((3,)),
         ],
         compiler_params=pltpu.CompilerParams(
-            collective_id=1, has_side_effects=True, vmem_limit_bytes=48 * 1024 * 1024),
-    )(partial)
+            collective_id=1, has_side_effects=True, vmem_limit_bytes=60 * 1024 * 1024),
+    )(near_local, far_local, partial, slab.reshape((-1,) + tile), near_tiles, far_left, far_right)
 
 
 def per_device(panel_values, near_tiles, far_left, far_right, near_rows, far_rows):
@@ -305,7 +325,7 @@
     far_local = far_rows - row_base
     slab = gather_slabs(panel_values, n_row, n_col)
     partial = local_products(near_local, far_local, near_tiles, far_left, far_right, slab, colcount, groups)
-    return scatter_sum(partial, n_row, n_col)
+    return scatter_sum(partial, slab, near_local, far_local, near_tiles, far_left, far_right, n_row, n_col)
 
 
 def solution(mesh):

time: 146 us -> 139 us (0.952)
  the two profiles are of different devices: /device:TPU:18 before, /device:TPU:2 now
where the time goes in v8:
time: 139 us; the launch traced here: 138 us
  Pallas kernels  133 us (96%)
  local copies, waits for them, and re-layouts  3.54 us (3%)
    pallas_call x1, Pallas kernels, scatter_sum(): pl.pallas_call(functools.partial(scatter_kernel, nr, nc), out_shape=jax.S...  63.5 us
    pallas_call x1, Pallas kernels, gather_slabs(): pl.pallas_call(functools.partial(gather_kernel, nr, nc), out_shape=jax.Sh...  52.8 us
    pallas_call x1, Pallas kernels, local_products(): pl.pallas_call(functools.partial(local_kernel, half), grid_spec=grid_spec...  17.1 us
    unnamed x7, local copies, waits for them, and re-layouts  3.54 us

profile of v8, /device:TPU:2, one launch (start us, length us, event | category | flops | bytes accessed | tf_op | source)
XLA Modules:
  0.0 138.3 jit_solution(17888646047305803313)
XLA Ops:
  0.0 0.7 broadcast_subtract_fusion.1.near_idx
  0.7 0.0 copy-start.1
  0.7 0.7 broadcast_subtract_fusion.far_idx
  1.3 0.0 copy-start.2
  1.3 52.8 %shard_map.64.slab_ref = bf16[4,8,256,256]{3,2,1,0:T(8,128)(2,1)} custom-call(bf16[256,256]{1,0:T(8,128)(2,1)} %x_ref.1), custom_call_target="tpu_custom_call" | custom-call | tf_op jit(solution)/shard_map/pallas_call | solution.py:167
  54.1 17.1 %shard_map.65.p_ref = f32[2,8,256,256]{3,2,1,0:T(8,128)S(1)} custom-call(s32[32]{0:T(128)S(1)} %broadcast_subtract_fusion.1.near_idx, s32[128]{0:T(128)S(1)} %broadcast_subtract_fusion.far_idx, bf16[32,256,256]{2,1,0:T(8,128)(2,1)} %tiles_hbm.1, bf16[128,64,256]{2,1,0:T(8,128)(2,1)} %left_hbm.1, bf16[128,64,256]{2,1,0:T(8,128)(2,1)} %right_hbm.1, ...), custom_call_target="tpu_custom_call" | custom-call | flops 3221225472 | bytes 16777216 | tf_op jit(solution)/shard_map/pallas_call | solution.py:55
  71.2 0.0 copy-done.1
  71.2 0.0 copy-done.2
  71.3 0.0 copy-start
  71.3 2.0 %copy-done = f32[2,8,256,256]{3,2,1,0:T(8,128)} copy-done((f32[2,8,256,256]{3,2,1,0:T(8,128)}, f32[2,8,256,256]{3,2,1,0:T(8,128)S(1)}, u32[]{:S(2)}) %copy-start) | copy-done | bytes 4194328
  73.2 63.5 %shard_map.66 = bf16[256,256]{1,0:T(8,128)(2,1)} custom-call(s32[32]{0:T(128)} %copy-done.1, s32[128]{0:T(128)} %copy-done.2, f32[2,8,256,256]{3,2,1,0:T(8,128)} %copy-done, bf16[32,256,256]{2,1,0:T(8,128)(2,1)} %bitcast.1, bf16[32,256,256]{2,1,0:T(8,128)(2,1)} %tiles_hbm.1, bf16[128,64,256]{2,1,0:T(8,128)(2,1)} %left_hbm.1, bf16[128,64,256]{2,1,0:T(8,128)(2,1)} %right_hbm.1), custom_call_target="tpu_custom_call" | custom-call | tf_op jit(solution)/shard_map/pallas_call | solution.py:285
  136.7 1.6 %copy.8 = bf16[256,256]{1,0:T(8,128)(2,1)} copy(bf16[256,256]{1,0:T(8,128)(2,1)} %shard_map.66) | data formatting | bytes 262144
Async XLA Ops:
  0.7 70.6 %copy-start.1 = (s32[32]{0:T(128)}, s32[32]{0:T(128)S(1)}, u32[]{:S(2)}) copy-start(s32[32]{0:T(128)S(1)} %broadcast_subtract_fusion.1.near_idx) | copy-start | bytes 388
  1.3 69.9 %copy-start.2 = (s32[128]{0:T(128)}, s32[128]{0:T(128)S(1)}, u32[]{:S(2)}) copy-start(s32[128]{0:T(128)S(1)} %broadcast_subtract_fusion.far_idx) | copy-start | bytes 1540
  71.3 2.0 %copy-start = (f32[2,8,256,256]{3,2,1,0:T(8,128)}, f32[2,8,256,256]{3,2,1,0:T(8,128)S(1)}, u32[]{:S(2)}) copy-start(f32[2,8,256,256]{3,2,1,0:T(8,128)S(1)} %shard_map.65.p_ref) | copy-start | bytes 12582916

commit v9 on v8

--- a/solution.py
+++ b/solution.py
@@ -16,44 +16,47 @@
 TN = (((0,), (0,)), ((), ()))
 
 
-def local_kernel(half, near_idx, far_idx, tiles_ref, left_ref, right_ref, slab_ref, out_ref):
-    k = pl.program_id(0)
+def local_kernel(half, per, near_idx, far_idx, tiles_ref, left_ref, right_ref, slab_ref, out_ref):
+    step = pl.program_id(0)
     base = slab_ref.shape[0] - 2
 
-    @pl.when(k == 0)
+    @pl.when(step == 0)
     def _():
         out_ref[...] = jnp.zeros_like(out_ref)
 
-    xc = slab_ref[base + k // half, lax.rem(k, half)]
-    tiles = tiles_ref[...].reshape(DPC * TILE, TILE)
-    near_f = jnp.dot(tiles, xc, preferred_element_type=jnp.float32)
-    for d in range(DPC):
-        r = near_idx[k * DPC + d]
-        out_ref[r // half, lax.rem(r, half)] += near_f[d * TILE:(d + 1) * TILE]
-    right = right_ref[...].reshape(LPC * RANK, TILE)
-    coef = jnp.dot(right, xc, preferred_element_type=jnp.float32).astype(jnp.bfloat16)
-    for d in range(LPC):
-        r = far_idx[k * LPC + d]
-        out_ref[r // half, lax.rem(r, half)] += lax.dot_general(
-            left_ref[d], coef[d * RANK:(d + 1) * RANK], TN, preferred_element_type=jnp.float32)
+    for kk in range(per):
+        k = step * per + kk
+        xc = slab_ref[base + k // half, lax.rem(k, half)]
+        tiles = tiles_ref[kk * DPC:(kk + 1) * DPC].reshape(DPC * TILE, TILE)
+        near_f = jnp.dot(tiles, xc, preferred_element_type=jnp.float32)
+        for d in range(DPC):
+            r = near_idx[k * DPC + d]
+            out_ref[r // half, lax.rem(r, half)] += near_f[d * TILE:(d + 1) * TILE]
+        right = right_ref[kk * LPC:(kk + 1) * LPC].reshape(LPC * RANK, TILE)
+        coef = jnp.dot(right, xc, preferred_element_type=jnp.float32).astype(jnp.bfloat16)
+        for d in range(LPC):
+            r = far_idx[k * LPC + d]
+            out_ref[r // half, lax.rem(r, half)] += lax.dot_general(
+                left_ref[kk * LPC + d], coef[d * RANK:(d + 1) * RANK], TN, preferred_element_type=jnp.float32)
 
 
 def local_products(near_local, far_local, near_tiles, far_left, far_right, slab, count, groups):
     half = slab.shape[1]
+    per = 4 if count % 4 == 0 else 1
     grid_spec = pltpu.PrefetchScalarGridSpec(
         num_scalar_prefetch=2,
-        grid=(count,),
+        grid=(count // per,),
         in_specs=[
-            pl.BlockSpec((DPC, TILE, TILE), lambda k, a, b: (k, 0, 0)),
-            pl.BlockSpec((LPC, RANK, TILE), lambda k, a, b: (k, 0, 0)),
-            pl.BlockSpec((LPC, RANK, TILE), lambda k, a, b: (k, 0, 0)),
+            pl.BlockSpec((per * DPC, TILE, TILE), lambda k, a, b: (k, 0, 0)),
+            pl.BlockSpec((per * LPC, RANK, TILE), lambda k, a, b: (k, 0, 0)),
+            pl.BlockSpec((per * LPC, RANK, TILE), lambda k, a, b: (k, 0, 0)),
             pl.BlockSpec(memory_space=pltpu.VMEM),
         ],
         out_specs=pl.BlockSpec(memory_space=pltpu.VMEM),
     )
     flops = 2 * TILE * TILE * NRHS * near_tiles.shape[0] + 2 * RANK * TILE * NRHS * far_left.shape[0] * 2
     return pl.pallas_call(
-        functools.partial(local_kernel, half),
+        functools.partial(local_kernel, half, per),
         grid_spec=grid_spec,
         out_shape=jax.ShapeDtypeStruct((groups // half, half, TILE, NRHS), jnp.float32),
         compiler_params=pltpu.CompilerParams(
@@ -104,11 +107,11 @@
     chip = j // 2
     base = nc // half
     mine = slab_ref.at[j // half, lax.rem(j, half)]
+    other = remote(x_ref, slab_ref.at[base + xh, z], ring_send.at[0], ring_recv.at[0], partner)
+    other.start()
     col_copies = [remote(x_ref, mine, col_send.at[n], col_recv.at[n], dev) for n, dev in enumerate(cols)]
     for c in col_copies:
         c.start()
-    other = remote(x_ref, slab_ref.at[base + xh, z], ring_send.at[0], ring_recv.at[0], partner)
-    other.start()
     own_row = pltpu.make_async_copy(x_ref, mine, local_sem.at[0])
     own_col = pltpu.make_async_copy(x_ref, slab_ref.at[base + xh, z], local_sem.at[1])
     own_row.start()

time: 139 us -> 124 us (0.89)
  Pallas kernels: 133 us -> 118 us
    pallas_call x1, Pallas kernels: 52.8 us -> 45.4 us  [gather_slabs(): pl.pallas_call(functools.partial(gather_kernel, nr, nc), out_shape=jax.Sh...]
    pallas_call x1, Pallas kernels: 17.1 us -> 12.2 us  [local_products(): pl.pallas_call(functools.partial(local_kernel, half, per), grid_spec=grid...]
    pallas_call x1, Pallas kernels: 63.5 us -> 60.9 us  [scatter_sum(): pl.pallas_call(functools.partial(scatter_kernel, nr, nc), out_shape=jax.S...]
where the time goes in v9:
time: 124 us; the launch traced here: 123 us
  Pallas kernels  118 us (95%)
  local copies, waits for them, and re-layouts  3.54 us (3%)
  other arithmetic  1.32 us (1%)
    pallas_call x1, Pallas kernels, scatter_sum(): pl.pallas_call(functools.partial(scatter_kernel, nr, nc), out_shape=jax.S...  60.9 us
    pallas_call x1, Pallas kernels, gather_slabs(): pl.pallas_call(functools.partial(gather_kernel, nr, nc), out_shape=jax.Sh...  45.4 us
    pallas_call x1, Pallas kernels, local_products(): pl.pallas_call(functools.partial(local_kernel, half, per), grid_spec=grid...  12.2 us
    unnamed x7, local copies, waits for them, and re-layouts  3.54 us

profile of v9, /device:TPU:2, one launch (start us, length us, event | category | flops | bytes accessed | tf_op | source)
XLA Modules:
  0.0 123.4 jit_solution(7047994330485736108)
XLA Ops:
  0.0 0.7 broadcast_subtract_fusion.1.near_idx
  0.7 0.0 copy-start.1
  0.7 0.7 broadcast_subtract_fusion.far_idx
  1.3 0.0 copy-start.2
  1.3 45.4 %shard_map.64.slab_ref = bf16[4,8,256,256]{3,2,1,0:T(8,128)(2,1)} custom-call(bf16[256,256]{1,0:T(8,128)(2,1)} %x_ref.1), custom_call_target="tpu_custom_call" | custom-call | tf_op jit(solution)/shard_map/pallas_call | solution.py:170
  46.7 12.2 %shard_map.65.p_ref = f32[2,8,256,256]{3,2,1,0:T(8,128)S(1)} custom-call(s32[32]{0:T(128)S(1)} %broadcast_subtract_fusion.1.near_idx, s32[128]{0:T(128)S(1)} %broadcast_subtract_fusion.far_idx, bf16[32,256,256]{2,1,0:T(8,128)(2,1)} %tiles_hbm.1, bf16[128,64,256]{2,1,0:T(8,128)(2,1)} %left_hbm.1, bf16[128,64,256]{2,1,0:T(8,128)(2,1)} %right_hbm.1, ...), custom_call_target="tpu_custom_call" | custom-call | flops 3221225472 | bytes 16777216 | tf_op jit(solution)/shard_map/pallas_call | solution.py:58
  58.9 0.0 copy-done.1
  59.0 0.0 copy-done.2
  59.0 0.0 copy-start
  59.0 2.0 %copy-done = f32[2,8,256,256]{3,2,1,0:T(8,128)} copy-done((f32[2,8,256,256]{3,2,1,0:T(8,128)}, f32[2,8,256,256]{3,2,1,0:T(8,128)S(1)}, u32[]{:S(2)}) %copy-start) | copy-done | bytes 4194328
  60.9 60.9 %shard_map.66 = bf16[256,256]{1,0:T(8,128)(2,1)} custom-call(s32[32]{0:T(128)} %copy-done.1, s32[128]{0:T(128)} %copy-done.2, f32[2,8,256,256]{3,2,1,0:T(8,128)} %copy-done, bf16[32,256,256]{2,1,0:T(8,128)(2,1)} %bitcast.1, bf16[32,256,256]{2,1,0:T(8,128)(2,1)} %tiles_hbm.1, bf16[128,64,256]{2,1,0:T(8,128)(2,1)} %left_hbm.1, bf16[128,64,256]{2,1,0:T(8,128)(2,1)} %right_hbm.1), custom_call_target="tpu_custom_call" | custom-call | tf_op jit(solution)/shard_map/pallas_call | solution.py:288
  121.8 1.6 %copy.8 = bf16[256,256]{1,0:T(8,128)(2,1)} copy(bf16[256,256]{1,0:T(8,128)(2,1)} %shard_map.66) | data formatting | bytes 262144
Async XLA Ops:
  0.7 58.3 %copy-start.1 = (s32[32]{0:T(128)}, s32[32]{0:T(128)S(1)}, u32[]{:S(2)}) copy-start(s32[32]{0:T(128)S(1)} %broadcast_subtract_fusion.1.near_idx) | copy-start | bytes 388
  1.3 57.6 %copy-start.2 = (s32[128]{0:T(128)}, s32[128]{0:T(128)S(1)}, u32[]{:S(2)}) copy-start(s32[128]{0:T(128)S(1)} %broadcast_subtract_fusion.far_idx) | copy-start | bytes 1540
  59.0 2.0 %copy-start = (f32[2,8,256,256]{3,2,1,0:T(8,128)}, f32[2,8,256,256]{3,2,1,0:T(8,128)S(1)}, u32[]{:S(2)}) copy-start(f32[2,8,256,256]{3,2,1,0:T(8,128)S(1)} %shard_map.65.p_ref) | copy-start | bytes 12582916

commit v10 on v9

--- a/solution.py
+++ b/solution.py
@@ -189,10 +189,24 @@
     i, j, half, xh, z, cols, right, left, partner = layout(nr, nc)
     cw = half // 2
     ccw = half - 1 - cw
-    loads = [pltpu.make_async_copy(src, dst, local_sem.at[n])
-             for n, (src, dst) in enumerate([(tiles_hbm, tiles_v), (right_hbm, right_v), (left_hbm, left_v)])]
-    for c in loads:
-        c.start()
+    need = []
+    for t in range(1, cw + 1):
+        need.append(lax.rem(z + cw + 1 - t, half))
+        if t <= ccw:
+            need.append(lax.rem(z + half - (ccw + 1 - t), half))
+    need.append(z)
+    loads = []
+    for p, target in enumerate(need):
+        group = []
+        for xhp in range(2):
+            k = xhp * half + target
+            for n, (src, dst, width) in enumerate(
+                    [(tiles_hbm, tiles_v, DPC), (right_hbm, right_v, LPC), (left_hbm, left_v, LPC)]):
+                span = pl.ds(k * width, width)
+                c = pltpu.make_async_copy(src.at[span], dst.at[span], local_sem.at[p, xhp, n])
+                c.start()
+                group.append(c)
+        loads.append(group)
     enter(cols + [right, left, partner])
     chips = nc // 2
     core = lax.rem(j, 2)
@@ -200,12 +214,12 @@
     mate = cols[-1]
     handed = [2 * lax.rem(chip + o, chips) + 1 - core for o in range(1, chips)] + [mate[1]]
     col_copies = [remote(p_ref.at[m // half, lax.rem(m, half)], pre.at[n], col_send.at[n], col_recv.at[n], mate) for n, m in enumerate(handed)]
-    for c in col_copies:
-        c.start()
     sends = []
     arrivals = {}
-    for c in loads:
-        c.wait()
+
+    def fetch(p):
+        for c in loads[p]:
+            c.wait()
 
     def back(xhp, target):
         k = xhp * half + target
@@ -231,6 +245,7 @@
             else:
                 target = lax.rem(z + half - (ccw + 1 - t), half)
                 slot, dev = cw + t - 1, left
+            fetch(len(arrivals))
             back(0, target)
             back(1, target)
             if t == 1:
@@ -255,8 +270,12 @@
     for n in range(max(cw, chips - 1)):
         if n < cw:
             ring_step(n + 1)
+        if n == 0:
+            for c in col_copies:
+                c.start()
         if n < chips - 1:
             col_step(n + 1)
+    fetch(len(need) - 1)
     back(0, z)
     back(1, z)
     col_copies[chips - 1].wait_recv()
@@ -310,7 +329,7 @@
             pltpu.SemaphoreType.DMA((nc - 1,)),
             pltpu.SemaphoreType.DMA((half,)),
             pltpu.SemaphoreType.DMA((half,)),
-            pltpu.SemaphoreType.DMA((3,)),
+            pltpu.SemaphoreType.DMA((half, 2, 3)),
         ],
         compiler_params=pltpu.CompilerParams(
             collective_id=1, has_side_effects=True, vmem_limit_bytes=60 * 1024 * 1024),

time: 124 us -> 126 us (1.016)
  Pallas kernels: 118 us -> 121 us
    pallas_call x1, Pallas kernels: 60.9 us -> 63.2 us  [scatter_sum(): pl.pallas_call(functools.partial(scatter_kernel, nr, nc), out_shape=jax.S...]
where the time goes in v10:
time: 126 us
  Pallas kernels  121 us (96%)
  local copies, waits for them, and re-layouts  3.54 us (3%)
  other arithmetic  1.32 us (1%)
    pallas_call x1, Pallas kernels, scatter_sum(): pl.pallas_call(functools.partial(scatter_kernel, nr, nc), out_shape=jax.S...  63.2 us
    pallas_call x1, Pallas kernels, gather_slabs(): pl.pallas_call(functools.partial(gather_kernel, nr, nc), out_shape=jax.Sh...  45.4 us
    pallas_call x1, Pallas kernels, local_products(): pl.pallas_call(functools.partial(local_kernel, half, per), grid_spec=grid...  12.2 us
    unnamed x7, local copies, waits for them, and re-layouts  3.54 us

profile of v10, /device:TPU:2, one launch (start us, length us, event | category | flops | bytes accessed | tf_op | source)
XLA Modules:
  0.0 125.7 jit_solution(1890781416122104527)
XLA Ops:
  0.0 0.7 broadcast_subtract_fusion.1.near_idx
  0.7 0.0 copy-start.1
  0.7 0.7 broadcast_subtract_fusion.far_idx
  1.3 0.0 copy-start.2
  1.3 45.4 %shard_map.64.slab_ref = bf16[4,8,256,256]{3,2,1,0:T(8,128)(2,1)} custom-call(bf16[256,256]{1,0:T(8,128)(2,1)} %x_ref.1), custom_call_target="tpu_custom_call" | custom-call | tf_op jit(solution)/shard_map/pallas_call | solution.py:170
  46.7 12.2 %shard_map.65.p_ref = f32[2,8,256,256]{3,2,1,0:T(8,128)S(1)} custom-call(s32[32]{0:T(128)S(1)} %broadcast_subtract_fusion.1.near_idx, s32[128]{0:T(128)S(1)} %broadcast_subtract_fusion.far_idx, bf16[32,256,256]{2,1,0:T(8,128)(2,1)} %tiles_hbm.1, bf16[128,64,256]{2,1,0:T(8,128)(2,1)} %left_hbm.1, bf16[128,64,256]{2,1,0:T(8,128)(2,1)} %right_hbm.1, ...), custom_call_target="tpu_custom_call" | custom-call | flops 3221225472 | bytes 16777216 | tf_op jit(solution)/shard_map/pallas_call | solution.py:58
  58.9 0.0 copy-done.1
  59.0 0.0 copy-done.2
  59.0 0.0 copy-start
  59.0 2.0 %copy-done = f32[2,8,256,256]{3,2,1,0:T(8,128)} copy-done((f32[2,8,256,256]{3,2,1,0:T(8,128)}, f32[2,8,256,256]{3,2,1,0:T(8,128)S(1)}, u32[]{:S(2)}) %copy-start) | copy-done | bytes 4194328
  60.9 63.2 %shard_map.66 = bf16[256,256]{1,0:T(8,128)(2,1)} custom-call(s32[32]{0:T(128)} %copy-done.1, s32[128]{0:T(128)} %copy-done.2, f32[2,8,256,256]{3,2,1,0:T(8,128)} %copy-done, bf16[32,256,256]{2,1,0:T(8,128)(2,1)} %bitcast.1, bf16[32,256,256]{2,1,0:T(8,128)(2,1)} %tiles_hbm.1, bf16[128,64,256]{2,1,0:T(8,128)(2,1)} %left_hbm.1, bf16[128,64,256]{2,1,0:T(8,128)(2,1)} %right_hbm.1), custom_call_target="tpu_custom_call" | custom-call | tf_op jit(solution)/shard_map/pallas_call | solution.py:307
  124.1 1.6 %copy.8 = bf16[256,256]{1,0:T(8,128)(2,1)} copy(bf16[256,256]{1,0:T(8,128)(2,1)} %shard_map.66) | data formatting | bytes 262144
Async XLA Ops:
  0.7 58.3 %copy-start.1 = (s32[32]{0:T(128)}, s32[32]{0:T(128)S(1)}, u32[]{:S(2)}) copy-start(s32[32]{0:T(128)S(1)} %broadcast_subtract_fusion.1.near_idx) | copy-start | bytes 388
  1.3 57.6 %copy-start.2 = (s32[128]{0:T(128)}, s32[128]{0:T(128)S(1)}, u32[]{:S(2)}) copy-start(s32[128]{0:T(128)S(1)} %broadcast_subtract_fusion.far_idx) | copy-start | bytes 1540
  59.0 2.0 %copy-start = (f32[2,8,256,256]{3,2,1,0:T(8,128)}, f32[2,8,256,256]{3,2,1,0:T(8,128)S(1)}, u32[]{:S(2)}) copy-start(f32[2,8,256,256]{3,2,1,0:T(8,128)S(1)} %shard_map.65.p_ref) | copy-start | bytes 12582916

commit v11 on v9

--- a/solution.py
+++ b/solution.py
@@ -221,28 +221,41 @@
         acc += lax.dot_general(rfac, far_t[...], TN, preferred_element_type=jnp.float32)
         b_buf[xhp, target] = acc
 
-    def ring_step(t):
-        for way in range(2):
-            if way == 1 and t > ccw:
-                continue
-            if way == 0:
-                target = lax.rem(z + cw + 1 - t, half)
-                slot, dev = t - 1, right
-            else:
-                target = lax.rem(z + half - (ccw + 1 - t), half)
-                slot, dev = cw + t - 1, left
+    h2 = TILE // 2
+    chains = [(right, cw, 1, 0), (left, ccw, -1, 0), (right, ccw, 1, h2), (left, cw, -1, h2)]
+    slots = {}
+    for t in range(1, cw + 1):
+        for c, (dev, length, sign, row) in enumerate(chains):
+            if t <= length:
+                slots[(c, t)] = len(slots)
+    ready = set()
+
+    def ensure(off):
+        if off % half not in ready:
+            ready.add(off % half)
+            target = lax.rem(z + off + half, half)
             back(0, target)
             back(1, target)
+
+    def ring_step(t):
+        for c, (dev, length, sign, row) in enumerate(chains):
+            if t > length:
+                continue
+            off = sign * (length + 1 - t)
+            ensure(off)
+            target = lax.rem(z + off + half, half)
+            slot = slots[(c, t)]
+            rows = pl.ds(row, h2)
             if t == 1:
-                src = b_buf.at[:, target]
+                src = b_buf.at[:, target, rows]
             else:
-                arrivals[(way, t - 1)].wait_recv()
-                ring_out[slot] = ring_in[slot - 1] + b_buf[:, target]
+                arrivals[(c, t - 1)].wait_recv()
+                ring_out[slot] = ring_in[slots[(c, t - 1)]] + b_buf[:, target, rows]
                 src = ring_out.at[slot]
-            c = remote(src, ring_in.at[slot], ring_send.at[slot], ring_recv.at[slot], dev)
-            c.start()
-            sends.append(c)
-            arrivals[(way, t)] = c
+            cp = remote(src, ring_in.at[slot], ring_send.at[slot], ring_recv.at[slot], dev)
+            cp.start()
+            sends.append(cp)
+            arrivals[(c, t)] = cp
 
     def col_step(o):
         dev = cols[o - 1]
@@ -257,14 +270,18 @@
             ring_step(n + 1)
         if n < chips - 1:
             col_step(n + 1)
-    back(0, z)
-    back(1, z)
+    ensure(0)
     col_copies[chips - 1].wait_recv()
-    arrivals[(0, cw)].wait_recv()
-    arrivals[(1, ccw)].wait_recv()
+    lasts = []
+    for c, (dev, length, sign, row) in enumerate(chains):
+        arrivals[(c, length)].wait_recv()
+        lasts.append(slots[(c, length)])
     away = 1 - xh
-    x_out[...] = ring_in[cw - 1, away] + ring_in[cw + ccw - 1, away] + b_buf[away, z]
-    cross = remote(x_out, x_in, ring_send.at[half - 1], ring_recv.at[half - 1], partner)
+    for half_rows, (p, q) in enumerate([(lasts[0], lasts[1]), (lasts[2], lasts[3])]):
+        rows = slice(half_rows * h2, (half_rows + 1) * h2)
+        x_out[rows] = ring_in[p, away] + ring_in[q, away] + b_buf[away, z, rows]
+    nsem = len(slots)
+    cross = remote(x_out, x_in, ring_send.at[nsem], ring_recv.at[nsem], partner)
     cross.start()
     for c in sends:
         c.wait_send()
@@ -273,7 +290,9 @@
     for c in col_copies[chips:]:
         c.wait_recv()
     cross.wait()
-    acc = ring_in[cw - 1, xh] + ring_in[cw + ccw - 1, xh] + b_buf[xh, z] + x_in[...] + p_ref[j // half, lax.rem(j, half)] + pre[chips - 1]
+    ring_sum = jnp.concatenate(
+        [ring_in[lasts[0], xh] + ring_in[lasts[1], xh], ring_in[lasts[2], xh] + ring_in[lasts[3], xh]], axis=0)
+    acc = ring_sum + b_buf[xh, z] + x_in[...] + p_ref[j // half, lax.rem(j, half)] + pre[chips - 1]
     for n in range(chips - 1):
         acc = acc + recv_f[n]
     out_ref[...] = acc.astype(out_ref.dtype)
@@ -302,14 +321,14 @@
             vmem((nc // 2 - 1,) + tile, jnp.float32),
             vmem((nc // 2,) + tile, jnp.float32),
             vmem((nc // 2 - 1,) + tile, jnp.float32),
-            vmem((steps, 2) + tile, jnp.float32),
-            vmem((steps, 2) + tile, jnp.float32),
+            vmem((2 * steps, 2, tile[0] // 2, tile[1]), jnp.float32),
+            vmem((2 * steps, 2, tile[0] // 2, tile[1]), jnp.float32),
             vmem(tile, jnp.float32),
             vmem(tile, jnp.float32),
             pltpu.SemaphoreType.DMA((nc - 1,)),
             pltpu.SemaphoreType.DMA((nc - 1,)),
-            pltpu.SemaphoreType.DMA((half,)),
-            pltpu.SemaphoreType.DMA((half,)),
+            pltpu.SemaphoreType.DMA((2 * steps + 1,)),
+            pltpu.SemaphoreType.DMA((2 * steps + 1,)),
             pltpu.SemaphoreType.DMA((3,)),
         ],
         compiler_params=pltpu.CompilerParams(

time: 124 us -> 125 us (level)
  Pallas kernels: 118 us -> 120 us
    pallas_call x1, Pallas kernels: 60.9 us -> 62.6 us  [scatter_sum(): pl.pallas_call(functools.partial(scatter_kernel, nr, nc), out_shape=jax.S...]
where the time goes in v11:
time: 125 us
  Pallas kernels  120 us (96%)
  local copies, waits for them, and re-layouts  3.54 us (3%)
  other arithmetic  1.32 us (1%)
    pallas_call x1, Pallas kernels, scatter_sum(): pl.pallas_call(functools.partial(scatter_kernel, nr, nc), out_shape=jax.S...  62.6 us
    pallas_call x1, Pallas kernels, gather_slabs(): pl.pallas_call(functools.partial(gather_kernel, nr, nc), out_shape=jax.Sh...  45.4 us
    pallas_call x1, Pallas kernels, local_products(): pl.pallas_call(functools.partial(local_kernel, half, per), grid_spec=grid...  12.2 us
    unnamed x7, local copies, waits for them, and re-layouts  3.54 us

profile of v11, /device:TPU:2, one launch (start us, length us, event | category | flops | bytes accessed | tf_op | source)
XLA Modules:
  0.0 125.1 jit_solution(10127706319751878387)
XLA Ops:
  0.0 0.7 broadcast_subtract_fusion.1.near_idx
  0.7 0.0 copy-start.1
  0.7 0.7 broadcast_subtract_fusion.far_idx
  1.3 0.0 copy-start.2
  1.3 45.4 %shard_map.64.slab_ref = bf16[4,8,256,256]{3,2,1,0:T(8,128)(2,1)} custom-call(bf16[256,256]{1,0:T(8,128)(2,1)} %x_ref.1), custom_call_target="tpu_custom_call" | custom-call | tf_op jit(solution)/shard_map/pallas_call | solution.py:170
  46.7 12.2 %shard_map.65.p_ref = f32[2,8,256,256]{3,2,1,0:T(8,128)S(1)} custom-call(s32[32]{0:T(128)S(1)} %broadcast_subtract_fusion.1.near_idx, s32[128]{0:T(128)S(1)} %broadcast_subtract_fusion.far_idx, bf16[32,256,256]{2,1,0:T(8,128)(2,1)} %tiles_hbm.1, bf16[128,64,256]{2,1,0:T(8,128)(2,1)} %left_hbm.1, bf16[128,64,256]{2,1,0:T(8,128)(2,1)} %right_hbm.1, ...), custom_call_target="tpu_custom_call" | custom-call | flops 3221225472 | bytes 16777216 | tf_op jit(solution)/shard_map/pallas_call | solution.py:58
  58.9 0.0 copy-done.1
  59.0 0.0 copy-done.2
  59.0 0.0 copy-start
  59.0 2.0 %copy-done = f32[2,8,256,256]{3,2,1,0:T(8,128)} copy-done((f32[2,8,256,256]{3,2,1,0:T(8,128)}, f32[2,8,256,256]{3,2,1,0:T(8,128)S(1)}, u32[]{:S(2)}) %copy-start) | copy-done | bytes 4194328
  60.9 62.6 %shard_map.66 = bf16[256,256]{1,0:T(8,128)(2,1)} custom-call(s32[32]{0:T(128)} %copy-done.1, s32[128]{0:T(128)} %copy-done.2, f32[2,8,256,256]{3,2,1,0:T(8,128)} %copy-done, bf16[32,256,256]{2,1,0:T(8,128)(2,1)} %bitcast.1, bf16[32,256,256]{2,1,0:T(8,128)(2,1)} %tiles_hbm.1, bf16[128,64,256]{2,1,0:T(8,128)(2,1)} %left_hbm.1, bf16[128,64,256]{2,1,0:T(8,128)(2,1)} %right_hbm.1), custom_call_target="tpu_custom_call" | custom-call | tf_op jit(solution)/shard_map/pallas_call | solution.py:307
  123.6 1.6 %copy.8 = bf16[256,256]{1,0:T(8,128)(2,1)} copy(bf16[256,256]{1,0:T(8,128)(2,1)} %shard_map.66) | data formatting | bytes 262144
Async XLA Ops:
  0.7 58.3 %copy-start.1 = (s32[32]{0:T(128)}, s32[32]{0:T(128)S(1)}, u32[]{:S(2)}) copy-start(s32[32]{0:T(128)S(1)} %broadcast_subtract_fusion.1.near_idx) | copy-start | bytes 388
  1.3 57.6 %copy-start.2 = (s32[128]{0:T(128)}, s32[128]{0:T(128)S(1)}, u32[]{:S(2)}) copy-start(s32[128]{0:T(128)S(1)} %broadcast_subtract_fusion.far_idx) | copy-start | bytes 1540
  59.0 2.0 %copy-start = (f32[2,8,256,256]{3,2,1,0:T(8,128)}, f32[2,8,256,256]{3,2,1,0:T(8,128)S(1)}, u32[]{:S(2)}) copy-start(f32[2,8,256,256]{3,2,1,0:T(8,128)S(1)} %shard_map.65.p_ref) | copy-start | bytes 12582916

commit v12 on v9

--- a/solution.py
+++ b/solution.py
@@ -313,7 +313,7 @@
             pltpu.SemaphoreType.DMA((3,)),
         ],
         compiler_params=pltpu.CompilerParams(
-            collective_id=1, has_side_effects=True, vmem_limit_bytes=60 * 1024 * 1024),
+            collective_id=1, has_side_effects=True, vmem_limit_bytes=40 * 1024 * 1024),
     )(near_local, far_local, partial, slab.reshape((-1,) + tile), near_tiles, far_left, far_right)
 
 

time: 124 us -> 119 us (0.960)
  local copies, waits for them, and re-layouts: 3.54 us -> 0.67 us
    unnamed x7 -> x5, local copies, waits for them, and re-layouts: 3.54 us -> 0.67 us
    pallas_call x1, Pallas kernels: 60.9 us -> 58.3 us  [scatter_sum(): pl.pallas_call(functools.partial(scatter_kernel, nr, nc), out_shape=jax.S...]
where the time goes in v12:
time: 119 us
  Pallas kernels  117 us (98%)
  other arithmetic  1.31 us (1%)
    pallas_call x1, Pallas kernels, scatter_sum(): pl.pallas_call(functools.partial(scatter_kernel, nr, nc), out_shape=jax.S...  58.3 us
    pallas_call x1, Pallas kernels, gather_slabs(): pl.pallas_call(functools.partial(gather_kernel, nr, nc), out_shape=jax.Sh...  45.4 us
    pallas_call x1, Pallas kernels, local_products(): pl.pallas_call(functools.partial(local_kernel, half, per), grid_spec=grid...  12.9 us

profile of v12, /device:TPU:2, one launch (start us, length us, event | category | flops | bytes accessed | tf_op | source)
XLA Modules:
  0.0 118.6 jit_solution(12180104081504610065)
XLA Ops:
  0.0 0.7 broadcast_subtract_fusion.1.near_idx
  0.7 0.7 broadcast_subtract_fusion.far_idx
  1.3 45.4 %shard_map.64.slab_ref = bf16[4,8,256,256]{3,2,1,0:T(8,128)(2,1)} custom-call(bf16[256,256]{1,0:T(8,128)(2,1)} %x_ref.1), custom_call_target="tpu_custom_call" | custom-call | tf_op jit(solution)/shard_map/pallas_call | solution.py:170
  46.7 0.0 copy-start
  46.7 0.0 copy-start.1
  46.7 12.9 %shard_map.65.p_ref = f32[2,8,256,256]{3,2,1,0:T(8,128)S(1)} custom-call(s32[32]{0:T(128)S(1)} %broadcast_subtract_fusion.1.near_idx, s32[128]{0:T(128)S(1)} %broadcast_subtract_fusion.far_idx, bf16[32,256,256]{2,1,0:T(8,128)(2,1)} %tiles_hbm.1, bf16[128,64,256]{2,1,0:T(8,128)(2,1)} %left_hbm.1, bf16[128,64,256]{2,1,0:T(8,128)(2,1)} %right_hbm.1, ...), custom_call_target="tpu_custom_call" | custom-call | flops 3221225472 | bytes 16777216 | tf_op jit(solution)/shard_map/pallas_call | solution.py:58
  59.6 0.0 copy-done
  59.6 0.0 copy-done.1
  59.7 58.3 %shard_map.66 = bf16[256,256]{1,0:T(8,128)(2,1)S(1)} custom-call(s32[32]{0:T(128)S(1)} %broadcast_subtract_fusion.1.near_idx, s32[128]{0:T(128)S(1)} %broadcast_subtract_fusion.far_idx, f32[2,8,256,256]{3,2,1,0:T(8,128)S(1)} %shard_map.65.p_ref, bf16[32,256,256]{2,1,0:T(8,128)(2,1)S(1)} %bitcast.1, bf16[32,256,256]{2,1,0:T(8,128)(2,1)S(1)} %copy-done.1, ...), custom_call_target="tpu_custom_call" | custom-call | tf_op jit(solution)/shard_map/pallas_call | solution.py:288
  118.0 0.7 copy.8
Async XLA Ops:
  46.7 12.9 %copy-start = (bf16[4,8,256,256]{3,2,1,0:T(8,128)(2,1)S(1)}, bf16[4,8,256,256]{3,2,1,0:T(8,128)(2,1)}, u32[]{:S(2)}) copy-start(bf16[4,8,256,256]{3,2,1,0:T(8,128)(2,1)} %shard_map.64.slab_ref) | copy-start | bytes 12582916
  46.7 12.9 %copy-start.1 = (bf16[32,256,256]{2,1,0:T(8,128)(2,1)S(1)}, bf16[32,256,256]{2,1,0:T(8,128)(2,1)}, u32[]{:S(2)}) copy-start(bf16[32,256,256]{2,1,0:T(8,128)(2,1)} %tiles_hbm.1) | copy-start | bytes 12582916

commit v13 on v12

--- a/solution.py
+++ b/solution.py
@@ -60,7 +60,7 @@
         grid_spec=grid_spec,
         out_shape=jax.ShapeDtypeStruct((groups // half, half, TILE, NRHS), jnp.float32),
         compiler_params=pltpu.CompilerParams(
-            dimension_semantics=("arbitrary",), vmem_limit_bytes=48 * 1024 * 1024
+            dimension_semantics=("arbitrary",), vmem_limit_bytes=24 * 1024 * 1024
         ),
         cost_estimate=pl.CostEstimate(flops=flops, bytes_accessed=16 * 1024 * 1024, transcendentals=0),
     )(near_local, far_local, near_tiles, far_left, far_right, slab)
@@ -179,7 +179,8 @@
             pltpu.SemaphoreType.DMA((half,)),
             pltpu.SemaphoreType.DMA((2,)),
         ],
-        compiler_params=pltpu.CompilerParams(collective_id=0, has_side_effects=True),
+        compiler_params=pltpu.CompilerParams(
+            collective_id=0, has_side_effects=True, vmem_limit_bytes=16 * 1024 * 1024),
     )(x)
 
 

time: 119 us -> 118 us (level)
  Pallas kernels: 117 us -> 110 us
  local copies, waits for them, and re-layouts: 0.67 us -> 5.94 us
    unnamed x5 -> x9, local copies, waits for them, and re-layouts: 0.67 us -> 5.94 us
    pallas_call x1, Pallas kernels: 12.9 us -> 8.75 us  [local_products(): pl.pallas_call(functools.partial(local_kernel, half, per), grid_spec=grid...]
    pallas_call x1, Pallas kernels: 45.4 us -> 43.2 us  [gather_slabs(): pl.pallas_call(functools.partial(gather_kernel, nr, nc), out_shape=jax.Sh...]
where the time goes in v13:
time: 118 us
  Pallas kernels  110 us (93%)
  local copies, waits for them, and re-layouts  5.94 us (5%)
  other arithmetic  1.63 us (1%)
    pallas_call x1, Pallas kernels, scatter_sum(): pl.pallas_call(functools.partial(scatter_kernel, nr, nc), out_shape=jax.S...  58.2 us
    pallas_call x1, Pallas kernels, gather_slabs(): pl.pallas_call(functools.partial(gather_kernel, nr, nc), out_shape=jax.Sh...  43.2 us
    pallas_call x1, Pallas kernels, local_products(): pl.pallas_call(functools.partial(local_kernel, half, per), grid_spec=grid...  8.75 us
    unnamed x9, local copies, waits for them, and re-layouts  5.94 us

profile of v13, /device:TPU:2, one launch (start us, length us, event | category | flops | bytes accessed | tf_op | source)
XLA Modules:
  0.0 117.8 jit_solution(725151756533994767)
XLA Ops:
  0.0 0.0 copy-start
  0.0 0.8 broadcast_subtract_fusion.1.near_idx
  0.8 0.8 broadcast_subtract_fusion.far_idx
  1.6 0.0 copy-start.3
  1.6 0.9 copy-done.3
  2.5 43.2 %shard_map.64.slab_ref = bf16[4,8,256,256]{3,2,1,0:T(8,128)(2,1)S(1)} custom-call(bf16[256,256]{1,0:T(8,128)(2,1)S(1)} %copy-done.3), custom_call_target="tpu_custom_call" | custom-call | tf_op jit(solution)/shard_map/pallas_call | solution.py:170
  45.8 0.0 copy-done
  45.8 0.0 copy-start.1
  45.8 2.2 %copy-done.1 = bf16[128,64,256]{2,1,0:T(8,128)(2,1)S(1)} copy-done((bf16[128,64,256]{2,1,0:T(8,128)(2,1)S(1)}, bf16[128,64,256]{2,1,0:T(8,128)(2,1)}, u32[]{:S(2)}) %copy-start.1) | copy-done | bytes 4194328
  48.0 0.0 copy-start.2
  48.0 2.2 %copy-done.2 = bf16[128,64,256]{2,1,0:T(8,128)(2,1)S(1)} copy-done((bf16[128,64,256]{2,1,0:T(8,128)(2,1)S(1)}, bf16[128,64,256]{2,1,0:T(8,128)(2,1)}, u32[]{:S(2)}) %copy-start.2) | copy-done | bytes 4194328
  50.2 8.8 %shard_map.65.p_ref = f32[2,8,256,256]{3,2,1,0:T(8,128)S(1)} custom-call(s32[32]{0:T(128)S(1)} %broadcast_subtract_fusion.1.near_idx, s32[128]{0:T(128)S(1)} %broadcast_subtract_fusion.far_idx, bf16[32,256,256]{2,1,0:T(8,128)(2,1)S(1)} %copy-done, bf16[128,64,256]{2,1,0:T(8,128)(2,1)S(1)} %copy-done.1, bf16[128,64,256]{2,1,0:T(8,128)(2,1)S(1)} %copy-done.2, ...), custom_call_target="tpu_custom_call" | custom-call | flops 3221225472 | bytes 16777216 | tf_op jit(solution)/shard_map/pallas_call | solution.py:58
  58.9 58.2 %shard_map.66 = bf16[256,256]{1,0:T(8,128)(2,1)S(1)} custom-call(s32[32]{0:T(128)S(1)} %broadcast_subtract_fusion.1.near_idx, s32[128]{0:T(128)S(1)} %broadcast_subtract_fusion.far_idx, f32[2,8,256,256]{3,2,1,0:T(8,128)S(1)} %shard_map.65.p_ref, bf16[32,256,256]{2,1,0:T(8,128)(2,1)S(1)} %bitcast.1, bf16[32,256,256]{2,1,0:T(8,128)(2,1)S(1)} %copy-done, ...), custom_call_target="tpu_custom_call" | custom-call | tf_op jit(solution)/shard_map/pallas_call | solution.py:289
  117.1 0.7 copy.8
Async XLA Ops:
  0.0 45.8 %copy-start = (bf16[32,256,256]{2,1,0:T(8,128)(2,1)S(1)}, bf16[32,256,256]{2,1,0:T(8,128)(2,1)}, u32[]{:S(2)}) copy-start(bf16[32,256,256]{2,1,0:T(8,128)(2,1)} %tiles_hbm.1) | copy-start | bytes 12582916
  1.6 0.9 copy-start.3
  45.8 2.2 %copy-start.1 = (bf16[128,64,256]{2,1,0:T(8,128)(2,1)S(1)}, bf16[128,64,256]{2,1,0:T(8,128)(2,1)}, u32[]{:S(2)}) copy-start(bf16[128,64,256]{2,1,0:T(8,128)(2,1)} %left_hbm.1) | copy-start | bytes 12582916
  48.0 2.2 %copy-start.2 = (bf16[128,64,256]{2,1,0:T(8,128)(2,1)S(1)}, bf16[128,64,256]{2,1,0:T(8,128)(2,1)}, u32[]{:S(2)}) copy-start(bf16[128,64,256]{2,1,0:T(8,128)(2,1)} %right_hbm.1) | copy-start | bytes 12582916

commit v14 on v13

--- a/solution.py
+++ b/solution.py
@@ -201,8 +201,6 @@
     mate = cols[-1]
     handed = [2 * lax.rem(chip + o, chips) + 1 - core for o in range(1, chips)] + [mate[1]]
     col_copies = [remote(p_ref.at[m // half, lax.rem(m, half)], pre.at[n], col_send.at[n], col_recv.at[n], mate) for n, m in enumerate(handed)]
-    for c in col_copies:
-        c.start()
     sends = []
     arrivals = {}
     for c in loads:
@@ -256,6 +254,9 @@
     for n in range(max(cw, chips - 1)):
         if n < cw:
             ring_step(n + 1)
+        if n == 0:
+            for c in col_copies:
+                c.start()
         if n < chips - 1:
             col_step(n + 1)
     back(0, z)

time: 118 us -> 118 us (level)
  no operation moved by 1% of the time
where the time goes in v14:
time: 118 us
  Pallas kernels  110 us (93%)
  local copies, waits for them, and re-layouts  5.94 us (5%)
  other arithmetic  1.63 us (1%)
    pallas_call x1, Pallas kernels, scatter_sum(): pl.pallas_call(functools.partial(scatter_kernel, nr, nc), out_shape=jax.S...  58.2 us
    pallas_call x1, Pallas kernels, gather_slabs(): pl.pallas_call(functools.partial(gather_kernel, nr, nc), out_shape=jax.Sh...  43.2 us
    pallas_call x1, Pallas kernels, local_products(): pl.pallas_call(functools.partial(local_kernel, half, per), grid_spec=grid...  8.75 us
    unnamed x9, local copies, waits for them, and re-layouts  5.94 us

profile of v14, /device:TPU:2, one launch (start us, length us, event | category | flops | bytes accessed | tf_op | source)
XLA Modules:
  0.0 117.8 jit_solution(16428533608487940333)
XLA Ops:
  0.0 0.0 copy-start
  0.0 0.8 broadcast_subtract_fusion.1.near_idx
  0.8 0.8 broadcast_subtract_fusion.far_idx
  1.6 0.0 copy-start.3
  1.6 0.9 copy-done.3
  2.5 43.2 %shard_map.64.slab_ref = bf16[4,8,256,256]{3,2,1,0:T(8,128)(2,1)S(1)} custom-call(bf16[256,256]{1,0:T(8,128)(2,1)S(1)} %copy-done.3), custom_call_target="tpu_custom_call" | custom-call | tf_op jit(solution)/shard_map/pallas_call | solution.py:170
  45.8 0.0 copy-done
  45.8 0.0 copy-start.1
  45.8 2.2 %copy-done.1 = bf16[128,64,256]{2,1,0:T(8,128)(2,1)S(1)} copy-done((bf16[128,64,256]{2,1,0:T(8,128)(2,1)S(1)}, bf16[128,64,256]{2,1,0:T(8,128)(2,1)}, u32[]{:S(2)}) %copy-start.1) | copy-done | bytes 4194328
  48.0 0.0 copy-start.2
  48.0 2.2 %copy-done.2 = bf16[128,64,256]{2,1,0:T(8,128)(2,1)S(1)} copy-done((bf16[128,64,256]{2,1,0:T(8,128)(2,1)S(1)}, bf16[128,64,256]{2,1,0:T(8,128)(2,1)}, u32[]{:S(2)}) %copy-start.2) | copy-done | bytes 4194328
  50.2 8.8 %shard_map.65.p_ref = f32[2,8,256,256]{3,2,1,0:T(8,128)S(1)} custom-call(s32[32]{0:T(128)S(1)} %broadcast_subtract_fusion.1.near_idx, s32[128]{0:T(128)S(1)} %broadcast_subtract_fusion.far_idx, bf16[32,256,256]{2,1,0:T(8,128)(2,1)S(1)} %copy-done, bf16[128,64,256]{2,1,0:T(8,128)(2,1)S(1)} %copy-done.1, bf16[128,64,256]{2,1,0:T(8,128)(2,1)S(1)} %copy-done.2, ...), custom_call_target="tpu_custom_call" | custom-call | flops 3221225472 | bytes 16777216 | tf_op jit(solution)/shard_map/pallas_call | solution.py:58
  58.9 58.2 %shard_map.66 = bf16[256,256]{1,0:T(8,128)(2,1)S(1)} custom-call(s32[32]{0:T(128)S(1)} %broadcast_subtract_fusion.1.near_idx, s32[128]{0:T(128)S(1)} %broadcast_subtract_fusion.far_idx, f32[2,8,256,256]{3,2,1,0:T(8,128)S(1)} %shard_map.65.p_ref, bf16[32,256,256]{2,1,0:T(8,128)(2,1)S(1)} %bitcast.1, bf16[32,256,256]{2,1,0:T(8,128)(2,1)S(1)} %copy-done, ...), custom_call_target="tpu_custom_call" | custom-call | tf_op jit(solution)/shard_map/pallas_call | solution.py:290
  117.1 0.7 copy.8
Async XLA Ops:
  0.0 45.8 %copy-start = (bf16[32,256,256]{2,1,0:T(8,128)(2,1)S(1)}, bf16[32,256,256]{2,1,0:T(8,128)(2,1)}, u32[]{:S(2)}) copy-start(bf16[32,256,256]{2,1,0:T(8,128)(2,1)} %tiles_hbm.1) | copy-start | bytes 12582916
  1.6 0.9 copy-start.3
  45.8 2.2 %copy-start.1 = (bf16[128,64,256]{2,1,0:T(8,128)(2,1)S(1)}, bf16[128,64,256]{2,1,0:T(8,128)(2,1)}, u32[]{:S(2)}) copy-start(bf16[128,64,256]{2,1,0:T(8,128)(2,1)} %left_hbm.1) | copy-start | bytes 12582916
  48.0 2.2 %copy-start.2 = (bf16[128,64,256]{2,1,0:T(8,128)(2,1)S(1)}, bf16[128,64,256]{2,1,0:T(8,128)(2,1)}, u32[]{:S(2)}) copy-start(bf16[128,64,256]{2,1,0:T(8,128)(2,1)} %right_hbm.1) | copy-start | bytes 12582916

commit v15 on v14

--- a/solution.py
+++ b/solution.py
@@ -42,7 +42,7 @@
 
 def local_products(near_local, far_local, near_tiles, far_left, far_right, slab, count, groups):
     half = slab.shape[1]
-    per = 4 if count % 4 == 0 else 1
+    per = 8 if count % 8 == 0 else 1
     grid_spec = pltpu.PrefetchScalarGridSpec(
         num_scalar_prefetch=2,
         grid=(count // per,),

time: 118 us -> 118 us (level)
  no operation moved by 1% of the time
where the time goes in v15:
time: 118 us
  Pallas kernels  110 us (93%)
  local copies, waits for them, and re-layouts  5.94 us (5%)
  other arithmetic  1.63 us (1%)
    pallas_call x1, Pallas kernels, scatter_sum(): pl.pallas_call(functools.partial(scatter_kernel, nr, nc), out_shape=jax.S...  58.2 us
    pallas_call x1, Pallas kernels, gather_slabs(): pl.pallas_call(functools.partial(gather_kernel, nr, nc), out_shape=jax.Sh...  43.2 us
    pallas_call x1, Pallas kernels, local_products(): pl.pallas_call(functools.partial(local_kernel, half, per), grid_spec=grid...  8.53 us
    unnamed x9, local copies, waits for them, and re-layouts  5.94 us

profile of v15, /device:TPU:2, one launch (start us, length us, event | category | flops | bytes accessed | tf_op | source)
XLA Modules:
  0.0 117.5 jit_solution(17345034806775238776)
XLA Ops:
  0.0 0.0 copy-start
  0.0 0.8 broadcast_subtract_fusion.1.near_idx
  0.8 0.8 broadcast_subtract_fusion.far_idx
  1.6 0.0 copy-start.3
  1.6 0.9 copy-done.3
  2.5 43.2 %shard_map.64.slab_ref = bf16[4,8,256,256]{3,2,1,0:T(8,128)(2,1)S(1)} custom-call(bf16[256,256]{1,0:T(8,128)(2,1)S(1)} %copy-done.3), custom_call_target="tpu_custom_call" | custom-call | tf_op jit(solution)/shard_map/pallas_call | solution.py:170
  45.8 0.0 copy-done
  45.8 0.0 copy-start.1
  45.8 2.2 %copy-done.1 = bf16[128,64,256]{2,1,0:T(8,128)(2,1)S(1)} copy-done((bf16[128,64,256]{2,1,0:T(8,128)(2,1)S(1)}, bf16[128,64,256]{2,1,0:T(8,128)(2,1)}, u32[]{:S(2)}) %copy-start.1) | copy-done | bytes 4194328
  48.0 0.0 copy-start.2
  48.0 2.2 %copy-done.2 = bf16[128,64,256]{2,1,0:T(8,128)(2,1)S(1)} copy-done((bf16[128,64,256]{2,1,0:T(8,128)(2,1)S(1)}, bf16[128,64,256]{2,1,0:T(8,128)(2,1)}, u32[]{:S(2)}) %copy-start.2) | copy-done | bytes 4194328
  50.2 8.5 %shard_map.65.p_ref = f32[2,8,256,256]{3,2,1,0:T(8,128)S(1)} custom-call(s32[32]{0:T(128)S(1)} %broadcast_subtract_fusion.1.near_idx, s32[128]{0:T(128)S(1)} %broadcast_subtract_fusion.far_idx, bf16[32,256,256]{2,1,0:T(8,128)(2,1)S(1)} %copy-done, bf16[128,64,256]{2,1,0:T(8,128)(2,1)S(1)} %copy-done.1, bf16[128,64,256]{2,1,0:T(8,128)(2,1)S(1)} %copy-done.2, ...), custom_call_target="tpu_custom_call" | custom-call | flops 3221225472 | bytes 16777216 | tf_op jit(solution)/shard_map/pallas_call | solution.py:58
  58.7 58.2 %shard_map.66 = bf16[256,256]{1,0:T(8,128)(2,1)S(1)} custom-call(s32[32]{0:T(128)S(1)} %broadcast_subtract_fusion.1.near_idx, s32[128]{0:T(128)S(1)} %broadcast_subtract_fusion.far_idx, f32[2,8,256,256]{3,2,1,0:T(8,128)S(1)} %shard_map.65.p_ref, bf16[32,256,256]{2,1,0:T(8,128)(2,1)S(1)} %bitcast.1, bf16[32,256,256]{2,1,0:T(8,128)(2,1)S(1)} %copy-done, ...), custom_call_target="tpu_custom_call" | custom-call | tf_op jit(solution)/shard_map/pallas_call | solution.py:290
  116.9 0.7 copy.8
Async XLA Ops:
  0.0 45.8 %copy-start = (bf16[32,256,256]{2,1,0:T(8,128)(2,1)S(1)}, bf16[32,256,256]{2,1,0:T(8,128)(2,1)}, u32[]{:S(2)}) copy-start(bf16[32,256,256]{2,1,0:T(8,128)(2,1)} %tiles_hbm.1) | copy-start | bytes 12582916
  1.6 0.9 copy-start.3
  45.8 2.2 %copy-start.1 = (bf16[128,64,256]{2,1,0:T(8,128)(2,1)S(1)}, bf16[128,64,256]{2,1,0:T(8,128)(2,1)}, u32[]{:S(2)}) copy-start(bf16[128,64,256]{2,1,0:T(8,128)(2,1)} %left_hbm.1) | copy-start | bytes 12582916
  48.0 2.2 %copy-start.2 = (bf16[128,64,256]{2,1,0:T(8,128)(2,1)S(1)}, bf16[128,64,256]{2,1,0:T(8,128)(2,1)}, u32[]{:S(2)}) copy-start(bf16[128,64,256]{2,1,0:T(8,128)(2,1)} %right_hbm.1) | copy-start | bytes 12582916

commit v16 on v15

--- a/solution.py
+++ b/solution.py
@@ -109,13 +109,13 @@
     mine = slab_ref.at[j // half, lax.rem(j, half)]
     other = remote(x_ref, slab_ref.at[base + xh, z], ring_send.at[0], ring_recv.at[0], partner)
     other.start()
+    own_col = pltpu.make_async_copy(x_ref, slab_ref.at[base + xh, z], local_sem.at[1])
+    own_col.start()
     col_copies = [remote(x_ref, mine, col_send.at[n], col_recv.at[n], dev) for n, dev in enumerate(cols)]
     for c in col_copies:
         c.start()
     own_row = pltpu.make_async_copy(x_ref, mine, local_sem.at[0])
-    own_col = pltpu.make_async_copy(x_ref, slab_ref.at[base + xh, z], local_sem.at[1])
     own_row.start()
-    own_col.start()
     mate = cols[-1]
     ring = []
     state = {}

time: 118 us -> 118 us (level)
  no operation moved by 1% of the time
where the time goes in v16:
time: 118 us
  Pallas kernels  110 us (93%)
  local copies, waits for them, and re-layouts  5.94 us (5%)
  other arithmetic  1.63 us (1%)
    pallas_call x1, Pallas kernels, scatter_sum(): pl.pallas_call(functools.partial(scatter_kernel, nr, nc), out_shape=jax.S...  58.3 us
    pallas_call x1, Pallas kernels, gather_slabs(): pl.pallas_call(functools.partial(gather_kernel, nr, nc), out_shape=jax.Sh...  43.2 us
    pallas_call x1, Pallas kernels, local_products(): pl.pallas_call(functools.partial(local_kernel, half, per), grid_spec=grid...  8.53 us
    unnamed x9, local copies, waits for them, and re-layouts  5.94 us

profile of v16, /device:TPU:2, one launch (start us, length us, event | category | flops | bytes accessed | tf_op | source)
XLA Modules:
  0.0 117.6 jit_solution(10694437540549846160)
XLA Ops:
  0.0 0.0 copy-start
  0.0 0.8 broadcast_subtract_fusion.1.near_idx
  0.8 0.8 broadcast_subtract_fusion.far_idx
  1.6 0.0 copy-start.3
  1.6 0.9 copy-done.3
  2.5 43.2 %shard_map.64.slab_ref = bf16[4,8,256,256]{3,2,1,0:T(8,128)(2,1)S(1)} custom-call(bf16[256,256]{1,0:T(8,128)(2,1)S(1)} %copy-done.3), custom_call_target="tpu_custom_call" | custom-call | tf_op jit(solution)/shard_map/pallas_call | solution.py:170
  45.8 0.0 copy-done
  45.8 0.0 copy-start.1
  45.8 2.2 %copy-done.1 = bf16[128,64,256]{2,1,0:T(8,128)(2,1)S(1)} copy-done((bf16[128,64,256]{2,1,0:T(8,128)(2,1)S(1)}, bf16[128,64,256]{2,1,0:T(8,128)(2,1)}, u32[]{:S(2)}) %copy-start.1) | copy-done | bytes 4194328
  48.0 0.0 copy-start.2
  48.0 2.2 %copy-done.2 = bf16[128,64,256]{2,1,0:T(8,128)(2,1)S(1)} copy-done((bf16[128,64,256]{2,1,0:T(8,128)(2,1)S(1)}, bf16[128,64,256]{2,1,0:T(8,128)(2,1)}, u32[]{:S(2)}) %copy-start.2) | copy-done | bytes 4194328
  50.2 8.5 %shard_map.65.p_ref = f32[2,8,256,256]{3,2,1,0:T(8,128)S(1)} custom-call(s32[32]{0:T(128)S(1)} %broadcast_subtract_fusion.1.near_idx, s32[128]{0:T(128)S(1)} %broadcast_subtract_fusion.far_idx, bf16[32,256,256]{2,1,0:T(8,128)(2,1)S(1)} %copy-done, bf16[128,64,256]{2,1,0:T(8,128)(2,1)S(1)} %copy-done.1, bf16[128,64,256]{2,1,0:T(8,128)(2,1)S(1)} %copy-done.2, ...), custom_call_target="tpu_custom_call" | custom-call | flops 3221225472 | bytes 16777216 | tf_op jit(solution)/shard_map/pallas_call | solution.py:58
  58.7 58.3 %shard_map.66 = bf16[256,256]{1,0:T(8,128)(2,1)S(1)} custom-call(s32[32]{0:T(128)S(1)} %broadcast_subtract_fusion.1.near_idx, s32[128]{0:T(128)S(1)} %broadcast_subtract_fusion.far_idx, f32[2,8,256,256]{3,2,1,0:T(8,128)S(1)} %shard_map.65.p_ref, bf16[32,256,256]{2,1,0:T(8,128)(2,1)S(1)} %bitcast.1, bf16[32,256,256]{2,1,0:T(8,128)(2,1)S(1)} %copy-done, ...), custom_call_target="tpu_custom_call" | custom-call | tf_op jit(solution)/shard_map/pallas_call | solution.py:290
  117.0 0.7 copy.8
Async XLA Ops:
  0.0 45.8 %copy-start = (bf16[32,256,256]{2,1,0:T(8,128)(2,1)S(1)}, bf16[32,256,256]{2,1,0:T(8,128)(2,1)}, u32[]{:S(2)}) copy-start(bf16[32,256,256]{2,1,0:T(8,128)(2,1)} %tiles_hbm.1) | copy-start | bytes 12582916
  1.6 0.9 copy-start.3
  45.8 2.2 %copy-start.1 = (bf16[128,64,256]{2,1,0:T(8,128)(2,1)S(1)}, bf16[128,64,256]{2,1,0:T(8,128)(2,1)}, u32[]{:S(2)}) copy-start(bf16[128,64,256]{2,1,0:T(8,128)(2,1)} %left_hbm.1) | copy-start | bytes 12582916
  48.0 2.2 %copy-start.2 = (bf16[128,64,256]{2,1,0:T(8,128)(2,1)S(1)}, bf16[128,64,256]{2,1,0:T(8,128)(2,1)}, u32[]{:S(2)}) copy-start(bf16[128,64,256]{2,1,0:T(8,128)(2,1)} %right_hbm.1) | copy-start | bytes 12582916
